TPU v7x, 256 devices: a whole 4x4x8 slice. The times are simulated.
256 devices in a mesh: row: 16 (over x_lo, y, core), col: 16 (over z, x_hi).
Axes of the slice: x: 4 (x_hi: 2, x_lo: 2; x = x_hi * 2 + x_lo), y: 4, z: 8, core: 2. Of those that a mesh axis runs over, the one named last changes fastest.
Arguments:
- green: bfloat16 [32768, 32768], P('row', 'col'), may hold values from -0.046875 to 0.046875
- mask: int32 [128, 128], P('row', 'col'), may hold values from 0 to 1, as said below
- probes: bfloat16 [32768, 256], P('col', 'row'), may hold values from -6 to 6
Outputs:
- sketch: float32 [32768, 256], P('row', 'col')
- adjoint: float32 [32768, 256], P('col', 'row')
Inputs may be any that keep to these rules, and one draw needn't show every extreme that they name: `mask`: block row i belongs to gauge i % 6 and time block i // 6; block column j to window j // 8. A block is 1 when its time block is no earlier than the window's onset plus a travel delay of its gauge and subfault block.
All inputs are finite; a program needn't handle non-finite values.
Results may differ from a plain program's by a relative error of at most 0.0022.
Values may be sent and summed in bfloat16 or wider, within the bound.
A program may use at most 128 MiB of HBM per device.

v0:
```python
import jax
import jax.numpy as jnp
from jax import lax
from jax.sharding import PartitionSpec as P


def local(green, mask, probes):
    row_blocks, col_blocks = mask.shape
    block_size = green.shape[0] // row_blocks
    shaped = green.reshape(row_blocks, block_size, col_blocks, block_size)
    tiles = (shaped * mask.astype(jnp.bfloat16)[:, None, :, None]).reshape(green.shape)
    partial_sketch = jnp.dot(
        tiles, lax.all_gather(probes, "row", axis=1, tiled=True), preferred_element_type=jnp.float32
    )
    summed = lax.psum(partial_sketch, "col")
    width_own = summed.shape[1] // lax.axis_size("col")
    own_sketch = lax.dynamic_slice_in_dim(summed, lax.axis_index("col") * width_own, width_own, 1)
    term = lax.dot_general(
        tiles,
        summed.astype(jnp.bfloat16),
        (((0,), (0,)), ((), ())),
        preferred_element_type=jnp.float32,
    )
    adjoint = lax.psum_scatter(term, "row", scatter_dimension=1, tiled=True)
    return (own_sketch, adjoint)


def solution(mesh):
    in_specs = (P("row", "col"), P("row", "col"), P("col", "row"))
    out_specs = (P("row", "col"), P("col", "row"))
    return jax.shard_map(local, mesh=mesh, in_specs=in_specs, out_specs=out_specs, check_vma=False)
```

profile of v0, /device:TPU:93, one launch (start us, length us, event | category | flops | bytes accessed | tf_op | source)
XLA Modules:
  0.0 296.7 jit_solution(3500955319090247931)
XLA Ops:
  7.2 0.0 all-gather.2.cloned.1.call-start
  7.2 0.7 all-gather.2.cloned.1.call-update
  7.9 0.0 all-reduce.2.cloned.1.call-start
  7.9 0.7 convert_element_type.6
  8.6 3.8 %mul.14 = bf16[8,256,8,256]{3,2,1,0:T(8,128)(2,1)} broadcast(bf16[8,8]{1,0:T(8,128)(2,1)S(1)} %convert_element_type.6), dimensions={0,2} | broadcast | bytes 8388736 | tf_op jit(solution)/shard_map/mul | solution.py:11
  12.5 10.3 %copy.6 = bf16[256,8,8,256]{3,1,2,0:T(8,128)(2,1)} copy(bf16[256,8,8,256]{3,2,1,0:T(8,128)(2,1)} %bitcast.7) | data formatting | bytes 16777216
  22.7 10.5 %mul.16 = bf16[2048,2048]{1,0:T(8,128)(2,1)} multiply(bf16[2048,2048]{1,0:T(8,128)(2,1)} %param.3, bf16[2048,2048]{1,0:T(8,128)(2,1)} %bitcast.6) | non-fusion elementwise | flops 4194304 | bytes 25165824 | tf_op jit(solution)/shard_map/mul | solution.py:11
  33.3 12.7 %all-gather.2.cloned.1.call-done = bf16[2048,256]{0,1:T(8,128)(2,1)} async-done(((bf16[2048,16]{0,1:T(8,128)(2,1)}), bf16[2048,256]{0,1:T(8,128)(2,1)}) %all-gather.2.cloned.1.call-update) | async-done | bytes 1048592 | tf_op jit(solution)/shard_map/all_gather | solution.py:13
  45.9 7.3 %fusion.2 = f32[2048,256]{1,0:T(8,128)} fusion(bf16[2048,2048]{1,0:T(8,128)(2,1)} %mul.16, bf16[2048,256]{0,1:T(8,128)(2,1)} %all-gather.2.cloned.1.call-done), kind=kOutput, calls=%fused_computation.3 | convolution fusion | flops 2147483648 | bytes 11534336 | tf_op jit(solution)/shard_map/dot_general | solution.py:12
  53.3 0.0 all-reduce.2.cloned.1.call-update
  53.3 0.0 reduce-scatter.2.cloned.1.call-start
  53.3 156.7 %all-reduce.2.cloned.1.call-done = f32[2048,256]{1,0:T(8,128)} async-done(((f32[2048,256]{1,0:T(8,128)}), f32[2048,256]{1,0:T(8,128)}) %all-reduce.2.cloned.1.call-update) | async-done | bytes 2097168 | tf_op jit(solution)/shard_map/psum | solution.py:15
  210.1 0.0 copy-start
  210.1 7.8 %fusion = f32[2048,256]{0,1:T(8,128)} fusion(bf16[2048,2048]{1,0:T(8,128)(2,1)} %mul.16, f32[2048,256]{1,0:T(8,128)} %all-reduce.2.cloned.1.call-done), kind=kOutput, calls=%fused_computation | convolution fusion | flops 2148007936 | bytes 12582912 | tf_op jit(solution)/shard_map/dot_general | solution.py:18
  217.9 0.0 reduce-scatter.2.cloned.1.call-update
  217.9 0.0 copy-done
  217.9 0.3 constant_dynamic-slice_fusion
  218.2 1.0 copy.5
  219.2 70.9 %reduce-scatter.2.cloned.1.call-done = f32[2048,16]{0,1:T(8,128)} async-done(((f32[2048,256]{0,1:T(8,128)}), f32[2048,16]{0,1:T(8,128)}) %reduce-scatter.2.cloned.1.call-update) | async-done | bytes 131088 | tf_op jit(solution)/shard_map/reduce_scatter | solution.py:24
Async XLA Ops:
  7.2 38.8 %all-gather.2.cloned.1.call-start = ((), (), s32[]{:S(2)}) async-start(), calls=%async_computation.1 | async-start | bytes 1114112 | tf_op jit(solution)/shard_map/all_gather | solution.py:13
  7.9 202.2 %all-reduce.2.cloned.1.call-start = ((), (), s32[]{:S(2)}) async-start(), calls=%async_computation.2 | async-start | bytes 4194304 | tf_op jit(solution)/shard_map/psum | solution.py:15
  53.3 236.9 %reduce-scatter.2.cloned.1.call-start = ((), (), s32[]{:S(2)}) async-start(), calls=%async_computation.3 | async-start | bytes 2228224 | tf_op jit(solution)/shard_map/reduce_scatter | solution.py:24
  210.1 7.8 %copy-start = (f32[2048,256]{1,0:T(8,128)S(1)}, f32[2048,256]{1,0:T(8,128)}, u32[]{:S(2)}) copy-start(f32[2048,256]{1,0:T(8,128)} %all-reduce.2.cloned.1.call-done) | copy-start | bytes 6291460
Sparse Core Ops, SparseCore 0:
  9.8 36.0 all-gather.1
  53.4 156.6 all-reduce.1
  218.0 72.1 reduce-scatter.1
where the time goes:
time: 300 us; the launch traced here: 297 us
  waiting for transfers between devices  241 us (80%)
  local copies, waits for them, and re-layouts  15.4 us (5%)
  matrix products  15.1 us (5%)
  between operations  13.8 us (5%)
  other arithmetic  11.2 us (4%)
    psum x1, waiting for transfers between devices, local(): summed = lax.psum(partial_sketch, 'col')  157 us
    reduce_scatter x1, waiting for transfers between devices, local(): adjoint = lax.psum_scatter(term, 'row', scatter_dimension=1, tiled=True)  70.9 us
    all_gather x1, waiting for transfers between devices, local(): lax.all_gather(probes, 'row', axis=1, tiled=True)  12.7 us
    unnamed x4, local copies, waits for them, and re-layouts  11.2 us
    mul x1, other arithmetic, local(): shaped * mask.astype(jnp.bfloat16)[:, None, :, None]  10.5 us
    dot_general x1, matrix products, local(): lax.dot_general(tiles, summed.astype(jnp.bfloat16), (((0,), (0,)), ((), (...  7.8 us
    dot_general x1, matrix products, local(): jnp.dot(tiles, lax.all_gather(probes, 'row', axis=1, tiled=True), preferr...  7.31 us
  transfers between devices with their start and end apart: 3, of which 3 were waited for; matrix products, arithmetic and copies ran while one was open for 9% of the time, Pallas kernels for 0%

commit v1 on v0

v1 whole, which is shorter than its diff:
```python
import jax
import jax.numpy as jnp
from jax import lax
from jax.sharding import PartitionSpec as P


def local(green, mask, probes):
    row_blocks, col_blocks = mask.shape
    block_size = green.shape[0] // row_blocks
    shaped = green.reshape(row_blocks, block_size, col_blocks, block_size)
    tiles = (shaped * mask.astype(jnp.bfloat16)[:, None, :, None]).reshape(green.shape)
    all_probes = lax.all_gather(probes, "row", axis=1, tiled=True)
    partial_sketch = jnp.dot(tiles, all_probes, preferred_element_type=jnp.float32)
    own_sketch = lax.psum_scatter(partial_sketch, "col", scatter_dimension=1, tiled=True)
    lowered = lax.all_gather(own_sketch.astype(jnp.bfloat16), "col", axis=1, tiled=True)
    term_t = lax.dot_general(
        lowered,
        tiles,
        (((0,), (0,)), ((), ())),
        preferred_element_type=jnp.float32,
    )
    adjoint_t = lax.psum_scatter(term_t, "row", scatter_dimension=0, tiled=True)
    return (own_sketch, adjoint_t.T)


def solution(mesh):
    in_specs = (P("row", "col"), P("row", "col"), P("col", "row"))
    out_specs = (P("row", "col"), P("col", "row"))
    return jax.shard_map(local, mesh=mesh, in_specs=in_specs, out_specs=out_specs, check_vma=False)
```

time: 300 us -> 420 us (1.40)
  waiting for transfers between devices: 241 us -> 361 us
    reduce_scatter x1 -> x2, waiting for transfers between devices: 70.9 us -> 269 us  [the longest x1 201 us: local(): lax.psum_scatter(partial_sketch, 'col', scatter_dimension=1, tiled=True)]
    psum x1 -> x0, waiting for transfers between devices: 157 us -> none  [local(): summed = lax.psum(partial_sketch, 'col')]
    all_gather x1 -> x2, waiting for transfers between devices: 12.7 us -> 91.2 us  [the longest x1 78.6 us: local(): lax.all_gather(own_sketch.astype(jnp.bfloat16), 'col', axis=1, tiled=True)]
    unnamed x4 -> x1, local copies, waits for them, and re-layouts: 11.2 us -> 10.3 us
  transfers between devices with their start and end apart: 3 -> 4, of which waited for: 3 -> 4; matrix products, arithmetic and copies ran while one was open for 9% -> 6% of each run, Pallas kernels for 0% -> 0%
where the time goes in v1:
time: 420 us; the launch traced here: 417 us
  waiting for transfers between devices  361 us (86%)
  matrix products  14.7 us (4%)
  local copies, waits for them, and re-layouts  14.1 us (3%)
  between operations  13.8 us (3%)
  other arithmetic  12.8 us (3%)
    reduce_scatter x1, waiting for transfers between devices, local(): lax.psum_scatter(partial_sketch, 'col', scatter_dimension=1, tiled=True)  201 us
    all_gather x1, waiting for transfers between devices, local(): lax.all_gather(own_sketch.astype(jnp.bfloat16), 'col', axis=1, tiled=True)  78.6 us
    reduce_scatter x1, waiting for transfers between devices, local(): adjoint_t = lax.psum_scatter(term_t, 'row', scatter_dimension=0, tiled=True)  67.9 us
    all_gather x1, waiting for transfers between devices, local(): all_probes = lax.all_gather(probes, 'row', axis=1, tiled=True)  12.7 us
    mul x1, other arithmetic, local(): shaped * mask.astype(jnp.bfloat16)[:, None, :, None]  10.5 us
    unnamed x1, local copies, waits for them, and re-layouts  10.3 us
  transfers between devices with their start and end apart: 4, of which 4 were waited for; matrix products, arithmetic and copies ran while one was open for 6% of the time, Pallas kernels for 0%

profile of v1, /device:TPU:93, one launch (start us, length us, event | category | flops | bytes accessed | tf_op | source)
XLA Modules:
  0.0 416.6 jit_solution(13793577123540415991)
XLA Ops:
  7.2 0.0 all-gather.3.cloned.1.call-start
  7.2 0.7 all-gather.3.cloned.1.call-update
  7.9 0.0 reduce-scatter.3.cloned.1.call-start
  7.9 0.7 convert_element_type.6
  8.6 3.8 mul.11
  12.5 10.3 %copy.5 = bf16[256,8,8,256]{3,1,2,0:T(8,128)(2,1)} copy(bf16[256,8,8,256]{3,2,1,0:T(8,128)(2,1)} %bitcast.9) | data formatting | bytes 16777216
  22.8 10.5 %mul.13 = bf16[2048,2048]{1,0:T(8,128)(2,1)} multiply(bf16[2048,2048]{1,0:T(8,128)(2,1)} %param.3, bf16[2048,2048]{1,0:T(8,128)(2,1)} %bitcast.8) | non-fusion elementwise | flops 4194304 | bytes 25165824 | tf_op jit(solution)/shard_map/mul | solution.py:11
  33.3 12.7 %all-gather.3.cloned.1.call-done = bf16[2048,256]{0,1:T(8,128)(2,1)} async-done(((bf16[2048,16]{0,1:T(8,128)(2,1)}), bf16[2048,256]{0,1:T(8,128)(2,1)}) %all-gather.3.cloned.1.call-update) | async-done | bytes 1048592 | tf_op jit(solution)/shard_map/all_gather | solution.py:12
  45.9 7.3 %fusion = f32[2048,256]{0,1:T(8,128)} fusion(bf16[2048,2048]{1,0:T(8,128)(2,1)} %mul.13, bf16[2048,256]{0,1:T(8,128)(2,1)} %all-gather.3.cloned.1.call-done), kind=kOutput, calls=%fused_computation | convolution fusion | flops 2147483648 | bytes 11534336 | tf_op jit(solution)/shard_map/dot_general | solution.py:13
  53.3 0.0 reduce-scatter.3.cloned.1.call-update
  53.3 0.0 all-gather.5.cloned.1.call-start
  53.4 201.2 %reduce-scatter.3.cloned.1.call-done = f32[2048,16]{0,1:T(8,128)} async-done(((f32[2048,256]{0,1:T(8,128)}), f32[2048,16]{0,1:T(8,128)}) %reduce-scatter.3.cloned.1.call-update) | async-done | bytes 131088 | tf_op jit(solution)/shard_map/reduce_scatter | solution.py:14
  254.6 1.5 convert_element_type.7
  256.1 0.0 all-gather.5.cloned.1.call-update
  256.1 0.0 reduce-scatter.5.cloned.1.call-start
  256.2 78.6 %all-gather.5.cloned.1.call-done = bf16[2048,256]{0,1:T(8,128)(2,1)} async-done(((bf16[2048,16]{0,1:T(8,128)(2,1)}), bf16[2048,256]{0,1:T(8,128)(2,1)}) %all-gather.5.cloned.1.call-update) | async-done | bytes 1048592 | tf_op jit(solution)/shard_map/all_gather | solution.py:15
  334.7 7.4 %fusion.1 = f32[256,2048]{1,0:T(8,128)} fusion(bf16[2048,256]{0,1:T(8,128)(2,1)} %all-gather.5.cloned.1.call-done, bf16[2048,2048]{1,0:T(8,128)(2,1)} %mul.13), kind=kOutput, calls=%fused_computation.1 | convolution fusion | flops 2147483648 | bytes 11534336 | tf_op jit(solution)/shard_map/dot_general | solution.py:16
  342.1 0.0 reduce-scatter.5.cloned.1.call-update
  342.2 67.9 %reduce-scatter.5.cloned.1.call-done = f32[16,2048]{1,0:T(8,128)} async-done(((f32[256,2048]{1,0:T(8,128)}), f32[16,2048]{1,0:T(8,128)}) %reduce-scatter.5.cloned.1.call-update) | async-done | bytes 131088 | tf_op jit(solution)/shard_map/reduce_scatter | solution.py:22
Async XLA Ops:
  7.2 38.8 %all-gather.3.cloned.1.call-start = ((), (), s32[]{:S(2)}) async-start(), calls=%async_computation.2 | async-start | bytes 1114112 | tf_op jit(solution)/shard_map/all_gather | solution.py:12
  7.9 246.7 %reduce-scatter.3.cloned.1.call-start = ((), (), s32[]{:S(2)}) async-start(), calls=%async_computation.3 | async-start | bytes 2228224 | tf_op jit(solution)/shard_map/reduce_scatter | solution.py:14
  53.3 281.4 %all-gather.5.cloned.1.call-start = ((), (), s32[]{:S(2)}) async-start(), calls=%async_computation.4 | async-start | bytes 1114112 | tf_op jit(solution)/shard_map/all_gather | solution.py:15
  256.1 153.9 %reduce-scatter.5.cloned.1.call-start = ((), (), s32[]{:S(2)}) async-start(), calls=%async_computation.5 | async-start | bytes 2228224 | tf_op jit(solution)/shard_map/reduce_scatter | solution.py:22
Sparse Core Ops, SparseCore 0:
  9.8 36.0 all-gather.2
  53.4 201.0 reduce-scatter.2
  257.7 76.9 all-gather.4
  342.3 67.7 reduce-scatter.4

commit v2 on v1

v2 whole, which is shorter than its diff:
```python
import functools

import jax
import jax.numpy as jnp
from jax import lax
from jax.experimental import pallas as pl
from jax.experimental.pallas import tpu as pltpu
from jax.sharding import PartitionSpec as P

MESH = pl.DeviceIdType.MESH


def _peer(axis, other, p):
    return (other, p) if axis == "col" else (p, other)


def _greet(axis, other, me, n):
    barrier = pltpu.get_barrier_semaphore()
    for d in range(1, n):
        peer = _peer(axis, other, lax.rem(me + d, n))
        pl.semaphore_signal(barrier, 1, device_id=peer, device_id_type=MESH)
    pl.semaphore_wait(barrier, n - 1)


def _rs_kernel(axis, other_axis, n, x_ref, o_ref, recv, send_sem, recv_sem):
    me = lax.axis_index(axis)
    other = lax.axis_index(other_axis)
    _greet(axis, other, me, n)
    copies = []
    for d in range(1, n):
        peer = lax.rem(me + d, n)
        copy = pltpu.make_async_remote_copy(
            src_ref=x_ref.at[peer],
            dst_ref=recv.at[d - 1],
            send_sem=send_sem.at[d - 1],
            recv_sem=recv_sem.at[d - 1],
            device_id=_peer(axis, other, peer),
            device_id_type=MESH,
        )
        copy.start()
        copies.append(copy)
    acc = x_ref[me]
    for d, copy in enumerate(copies):
        copy.wait_recv()
        acc = acc + recv[d]
    for copy in copies:
        copy.wait_send()
    o_ref[...] = acc


def _ag_kernel(axis, other_axis, n, x_ref, o_ref, recv, send_sem, recv_sem):
    me = lax.axis_index(axis)
    other = lax.axis_index(other_axis)
    _greet(axis, other, me, n)
    copies = []
    for d in range(1, n):
        peer = lax.rem(me + d, n)
        copy = pltpu.make_async_remote_copy(
            src_ref=x_ref,
            dst_ref=recv.at[d - 1],
            send_sem=send_sem.at[d - 1],
            recv_sem=recv_sem.at[d - 1],
            device_id=_peer(axis, other, peer),
            device_id_type=MESH,
        )
        copy.start()
        copies.append(copy)
    o_ref[me] = x_ref[...]
    for d, copy in enumerate(copies):
        copy.wait_recv()
        o_ref[lax.rem(me + n - 1 - d, n)] = recv[d]
    for copy in copies:
        copy.wait_send()


def _reduce_scatter(x, axis, other_axis, collective_id):
    n, rows, width = x.shape
    return pl.pallas_call(
        functools.partial(_rs_kernel, axis, other_axis, n),
        out_shape=jax.ShapeDtypeStruct((rows, width), x.dtype),
        in_specs=[pl.BlockSpec(memory_space=pltpu.VMEM)],
        out_specs=pl.BlockSpec(memory_space=pltpu.VMEM),
        scratch_shapes=[
            pltpu.VMEM((n - 1, rows, width), x.dtype),
            pltpu.SemaphoreType.DMA((n - 1,)),
            pltpu.SemaphoreType.DMA((n - 1,)),
        ],
        compiler_params=pltpu.CompilerParams(collective_id=collective_id, has_side_effects=True),
    )(x)


def _all_gather(x, axis, other_axis, n, collective_id):
    rows, width = x.shape
    return pl.pallas_call(
        functools.partial(_ag_kernel, axis, other_axis, n),
        out_shape=jax.ShapeDtypeStruct((n, rows, width), x.dtype),
        in_specs=[pl.BlockSpec(memory_space=pltpu.VMEM)],
        out_specs=pl.BlockSpec(memory_space=pltpu.VMEM),
        scratch_shapes=[
            pltpu.VMEM((n - 1, rows, width), x.dtype),
            pltpu.SemaphoreType.DMA((n - 1,)),
            pltpu.SemaphoreType.DMA((n - 1,)),
        ],
        compiler_params=pltpu.CompilerParams(collective_id=collective_id, has_side_effects=True),
    )(x)


def local(green, mask, probes):
    n_row = lax.axis_size("row")
    n_col = lax.axis_size("col")
    row_blocks, col_blocks = mask.shape
    block_size = green.shape[0] // row_blocks
    shaped = green.reshape(row_blocks, block_size, col_blocks, block_size)
    tiles = (shaped * mask.astype(jnp.bfloat16)[:, None, :, None]).reshape(green.shape)
    all_probes = lax.all_gather(probes, "row", axis=1, tiled=True)
    k = all_probes.shape[1]
    partial_t = jnp.dot(tiles, all_probes, preferred_element_type=jnp.float32).T
    sketch_t = _reduce_scatter(partial_t.reshape(n_col, k // n_col, -1), "col", "row", 0)
    lowered_t = _all_gather(sketch_t.astype(jnp.bfloat16), "col", "row", n_col, 1).reshape(k, -1)
    term_t = jnp.dot(lowered_t, tiles, preferred_element_type=jnp.float32)
    adjoint_t = _reduce_scatter(term_t.reshape(n_row, k // n_row, -1), "row", "col", 2)
    return (sketch_t.T, adjoint_t.T)


def solution(mesh):
    in_specs = (P("row", "col"), P("row", "col"), P("col", "row"))
    out_specs = (P("row", "col"), P("col", "row"))
    return jax.shard_map(local, mesh=mesh, in_specs=in_specs, out_specs=out_specs, check_vma=False)
```

time: 420 us -> 206 us (0.49)
  waiting for transfers between devices: 361 us -> 23.9 us
  Pallas kernels: 0 us -> 129 us
  other arithmetic: 12.8 us -> 2.23 us
  matrix products: 14.7 us -> 19.6 us
    reduce_scatter x2 -> x0, waiting for transfers between devices: 269 us -> none  [the longest x1 201 us: local(): lax.psum_scatter(partial_sketch, 'col', scatter_dimension=1, tiled=True)]
    pallas_call x0 -> x3, Pallas kernels: none -> 129 us  [the longest x2 98.4 us: _reduce_scatter(): pl.pallas_call(functools.partial(_rs_kernel, axis, other_axis, n), out_sh...]
    all_gather x1 -> x0, waiting for transfers between devices: 78.6 us -> none  [local(): lax.all_gather(own_sketch.astype(jnp.bfloat16), 'col', axis=1, tiled=True)]
    all_gather x1, waiting for transfers between devices: 12.7 us -> 23.2 us  [local(): all_probes = lax.all_gather(probes, 'row', axis=1, tiled=True)]
    mul x1 -> x0, other arithmetic: 10.5 us -> none  [local(): shaped * mask.astype(jnp.bfloat16)[:, None, :, None]]
    dot_general x2, matrix products: 14.7 us -> 19.6 us  [the longest x1 9.8 us: local(): term_t = jnp.dot(lowered_t, tiles, preferred_element_type=jnp.float32)]
    unnamed x1 -> x5, local copies, waits for them, and re-layouts: 10.3 us -> 12.5 us
  transfers between devices with their start and end apart: 4 -> 1, of which waited for: 4 -> 1; matrix products, arithmetic and copies ran while one was open for 6% -> 7% of each run, Pallas kernels for 0% -> 0%
where the time goes in v2:
time: 206 us; the launch traced here: 205 us
  Pallas kernels  129 us (63%)
  waiting for transfers between devices  23.9 us (12%)
  matrix products  19.6 us (10%)
  local copies, waits for them, and re-layouts  16.3 us (8%)
  between operations  14.1 us (7%)
  other arithmetic  2.23 us (1%)
    pallas_call x2, Pallas kernels, _reduce_scatter(): pl.pallas_call(functools.partial(_rs_kernel, axis, other_axis, n), out_sh...  98.4 us
    pallas_call x1, Pallas kernels, _all_gather(): pl.pallas_call(functools.partial(_ag_kernel, axis, other_axis, n), out_sh...  30.7 us
    all_gather x1, waiting for transfers between devices, local(): all_probes = lax.all_gather(probes, 'row', axis=1, tiled=True)  23.2 us
    unnamed x5, local copies, waits for them, and re-layouts  12.5 us
    dot_general x1, matrix products, local(): term_t = jnp.dot(lowered_t, tiles, preferred_element_type=jnp.float32)  9.8 us
    dot_general x1, matrix products, local(): partial_t = jnp.dot(tiles, all_probes, preferred_element_type=jnp.float32).T  9.76 us
  transfers between devices with their start and end apart: 1, of which 1 were waited for; matrix products, arithmetic and copies ran while one was open for 7% of the time, Pallas kernels for 0%

profile of v2, /device:TPU:93, one launch (start us, length us, event | category | flops | bytes accessed | tf_op | source)
XLA Modules:
  0.0 205.3 jit_solution(14423694529240356062)
XLA Ops:
  7.2 0.0 all-gather.2.cloned.1.call-start
  7.2 0.7 all-gather.2.cloned.1.call-update
  7.9 0.7 convert_element_type.6
  8.6 3.8 %mul.11 = bf16[8,256,8,256]{3,2,1,0:T(8,128)(2,1)} broadcast(bf16[8,8]{1,0:T(8,128)(2,1)S(1)} %convert_element_type.6), dimensions={0,2} | broadcast | bytes 8388736 | tf_op jit(solution)/shard_map/mul | solution.py:114
  12.4 10.3 %copy.5 = bf16[256,8,8,256]{3,1,2,0:T(8,128)(2,1)} copy(bf16[256,8,8,256]{3,2,1,0:T(8,128)(2,1)} %bitcast.13) | data formatting | bytes 16777216
  22.7 23.2 %all-gather.2.cloned.1.call-done = bf16[2048,256]{0,1:T(8,128)(2,1)} async-done(((bf16[2048,16]{0,1:T(8,128)(2,1)}), bf16[2048,256]{0,1:T(8,128)(2,1)}) %all-gather.2.cloned.1.call-update) | async-done | bytes 1048592 | tf_op jit(solution)/shard_map/all_gather | solution.py:115
  45.9 9.8 %fusion.3 = f32[2048,256]{0,1:T(8,128)} fusion(bf16[2048,256]{0,1:T(8,128)(2,1)} %all-gather.2.cloned.1.call-done, bf16[2048,2048]{1,0:T(8,128)(2,1)} %param.3, bf16[2048,2048]{1,0:T(8,128)(2,1)} %bitcast.14), kind=kOutput, calls=%fused_computation.3 | convolution fusion | flops 2151677952 | bytes 19922944 | tf_op jit(solution)/shard_map/dot_general | solution.py:117
  55.7 57.0 %shard_map.50 = f32[16,2048]{1,0:T(8,128)} custom-call(f32[16,16,2048]{2,1,0:T(8,128)} %bitcast.16), custom_call_target="tpu_custom_call" | custom-call | tf_op jit(solution)/shard_map/pallas_call | solution.py:78
  112.8 1.5 convert_element_type.7.x_ref
  114.3 30.7 %shard_map.51 = bf16[16,16,2048]{2,1,0:T(8,128)(2,1)} custom-call(bf16[16,2048]{1,0:T(8,128)(2,1)} %convert_element_type.7.x_ref), custom_call_target="tpu_custom_call" | custom-call | tf_op jit(solution)/shard_map/pallas_call | solution.py:94
  145.0 0.0 copy-start
  145.1 9.8 %fusion.x_ref = f32[16,16,2048]{2,1,0:T(8,128)} fusion(bf16[16,16,2048]{2,1,0:T(8,128)(2,1)} %shard_map.51, bf16[2048,2048]{1,0:T(8,128)(2,1)} %param.3, bf16[2048,2048]{1,0:T(8,128)(2,1)} %bitcast.15), kind=kOutput, calls=%fused_computation | convolution fusion | flops 2151677952 | bytes 19922944 | tf_op jit(solution)/shard_map/dot_general | solution.py:120
  154.9 41.4 %shard_map.52 = f32[16,2048]{1,0:T(8,128)} custom-call(f32[16,16,2048]{2,1,0:T(8,128)} %fusion.x_ref), custom_call_target="tpu_custom_call" | custom-call | tf_op jit(solution)/shard_map/pallas_call | solution.py:78
  196.2 0.0 copy-done
  196.2 0.7 copy.8
  196.9 1.6 copy.9
Async XLA Ops:
  7.2 38.8 %all-gather.2.cloned.1.call-start = ((), (), s32[]{:S(2)}) async-start(), calls=%async_computation | async-start | bytes 1114112 | tf_op jit(solution)/shard_map/all_gather | solution.py:115
  145.0 51.2 %copy-start = (f32[16,2048]{1,0:T(8,128)S(1)}, f32[16,2048]{1,0:T(8,128)}, u32[]{:S(2)}) copy-start(f32[16,2048]{1,0:T(8,128)} %shard_map.50) | copy-start | bytes 393220
Sparse Core Ops, SparseCore 0:
  9.8 36.0 all-gather.1

commit v3 on v2

--- a/solution.py
+++ b/solution.py
@@ -105,19 +105,81 @@
     )(x)
 
 
+def _sketch_kernel(nb, bs, mask_ref, g_ref, p_ref, o_ref):
+    i = pl.program_id(0)
+    o_ref[...] = jnp.zeros_like(o_ref)
+    for j in range(nb):
+        @pl.when(mask_ref[i, j] != 0)
+        def _():
+            o_ref[...] += lax.dot_general(
+                p_ref[:, j * bs:(j + 1) * bs],
+                g_ref[:, j * bs:(j + 1) * bs],
+                (((1,), (1,)), ((), ())),
+                preferred_element_type=jnp.float32,
+            )
+
+
+def _adjoint_kernel(nb, bs, mask_ref, l_ref, g_ref, o_ref):
+    j = pl.program_id(0)
+    o_ref[...] = jnp.zeros_like(o_ref)
+    for i in range(nb):
+        @pl.when(mask_ref[i, j] != 0)
+        def _():
+            o_ref[...] += jnp.dot(
+                l_ref[:, i * bs:(i + 1) * bs],
+                g_ref[i * bs:(i + 1) * bs, :],
+                preferred_element_type=jnp.float32,
+            )
+
+
+def _sketch_partial(mask, green, probes_t):
+    rb, cb = mask.shape
+    bs = green.shape[0] // rb
+    k = probes_t.shape[0]
+    return pl.pallas_call(
+        functools.partial(_sketch_kernel, cb, bs),
+        out_shape=jax.ShapeDtypeStruct((k, green.shape[0]), jnp.float32),
+        grid_spec=pltpu.PrefetchScalarGridSpec(
+            num_scalar_prefetch=1,
+            grid=(rb,),
+            in_specs=[
+                pl.BlockSpec((bs, green.shape[1]), lambda i, m: (i, 0)),
+                pl.BlockSpec((k, green.shape[1]), lambda i, m: (0, 0)),
+            ],
+            out_specs=pl.BlockSpec((k, bs), lambda i, m: (0, i)),
+        ),
+    )(mask, green, probes_t)
+
+
+def _adjoint_partial(mask, lowered_t, green):
+    rb, cb = mask.shape
+    bs = green.shape[0] // rb
+    k = lowered_t.shape[0]
+    return pl.pallas_call(
+        functools.partial(_adjoint_kernel, rb, bs),
+        out_shape=jax.ShapeDtypeStruct((k, green.shape[1]), jnp.float32),
+        grid_spec=pltpu.PrefetchScalarGridSpec(
+            num_scalar_prefetch=1,
+            grid=(cb,),
+            in_specs=[
+                pl.BlockSpec((k, green.shape[0]), lambda j, m: (0, 0)),
+                pl.BlockSpec((green.shape[0], bs), lambda j, m: (0, j)),
+            ],
+            out_specs=pl.BlockSpec((k, bs), lambda j, m: (0, j)),
+        ),
+    )(mask, lowered_t, green)
+
+
 def local(green, mask, probes):
     n_row = lax.axis_size("row")
     n_col = lax.axis_size("col")
-    row_blocks, col_blocks = mask.shape
-    block_size = green.shape[0] // row_blocks
-    shaped = green.reshape(row_blocks, block_size, col_blocks, block_size)
-    tiles = (shaped * mask.astype(jnp.bfloat16)[:, None, :, None]).reshape(green.shape)
-    all_probes = lax.all_gather(probes, "row", axis=1, tiled=True)
-    k = all_probes.shape[1]
-    partial_t = jnp.dot(tiles, all_probes, preferred_element_type=jnp.float32).T
+    probes_t = _all_gather(probes.T, "row", "col", n_row, 3)
+    k = probes_t.shape[0] * probes_t.shape[1]
+    probes_t = probes_t.reshape(k, -1)
+    partial_t = _sketch_partial(mask, green, probes_t)
     sketch_t = _reduce_scatter(partial_t.reshape(n_col, k // n_col, -1), "col", "row", 0)
     lowered_t = _all_gather(sketch_t.astype(jnp.bfloat16), "col", "row", n_col, 1).reshape(k, -1)
-    term_t = jnp.dot(lowered_t, tiles, preferred_element_type=jnp.float32)
+    term_t = _adjoint_partial(mask, lowered_t, green)
     adjoint_t = _reduce_scatter(term_t.reshape(n_row, k // n_row, -1), "row", "col", 2)
     return (sketch_t.T, adjoint_t.T)
 

time: 206 us -> 191 us (0.927)
  Pallas kernels: 129 us -> 186 us
  waiting for transfers between devices: 23.9 us -> 0 us
  matrix products: 19.6 us -> 0 us
  local copies, waits for them, and re-layouts: 16.3 us -> 2.23 us
  between operations: 14.1 us -> 0.67 us
    pallas_call x0 -> x2, Pallas kernels: none -> 33.1 us  [the longest x1 17.7 us: _sketch_partial(): pl.pallas_call(functools.partial(_sketch_kernel, cb, bs), out_shape=jax.S...]
    pallas_call x1 -> x2, Pallas kernels: 30.7 us -> 55.1 us  [_all_gather(): pl.pallas_call(functools.partial(_ag_kernel, axis, other_axis, n), out_sh...]
    all_gather x1 -> x0, waiting for transfers between devices: 23.2 us -> none  [local(): all_probes = lax.all_gather(probes, 'row', axis=1, tiled=True)]
    dot_general x2 -> x0, matrix products: 19.6 us -> none  [the longest x1 9.8 us: local(): term_t = jnp.dot(lowered_t, tiles, preferred_element_type=jnp.float32)]
    unnamed x5 -> x4, local copies, waits for them, and re-layouts: 12.5 us -> 2.23 us
    mul x1 -> x0, local copies, waits for them, and re-layouts: 3.83 us -> none  [local(): shaped * mask.astype(jnp.bfloat16)[:, None, :, None]]
  transfers between devices with their start and end apart: 1 -> 0, of which waited for: 1 -> 0; matrix products, arithmetic and copies ran while one was open for 7% -> 0% of each run, Pallas kernels for 0% -> 0%
where the time goes in v3:
time: 191 us; the launch traced here: 190 us
  Pallas kernels  186 us (97%)
  local copies, waits for them, and re-layouts  2.23 us (1%)
    pallas_call x2, Pallas kernels, _reduce_scatter(): pl.pallas_call(functools.partial(_rs_kernel, axis, other_axis, n), out_sh...  97.6 us
    pallas_call x2, Pallas kernels, _all_gather(): pl.pallas_call(functools.partial(_ag_kernel, axis, other_axis, n), out_sh...  55.1 us
    pallas_call x1, Pallas kernels, _sketch_partial(): pl.pallas_call(functools.partial(_sketch_kernel, cb, bs), out_shape=jax.S...  17.7 us
    pallas_call x1, Pallas kernels, _adjoint_partial(): pl.pallas_call(functools.partial(_adjoint_kernel, rb, bs), out_shape=jax....  15.4 us

profile of v3, /device:TPU:93, one launch (start us, length us, event | category | flops | bytes accessed | tf_op | source)
XLA Modules:
  0.0 190.2 jit_solution(4832702435114463380)
XLA Ops:
  0.6 21.7 %shard_map.50 = bf16[16,16,2048]{2,1,0:T(8,128)(2,1)} custom-call(bf16[16,2048]{1,0:T(8,128)(2,1)} %bitcast.13), custom_call_target="tpu_custom_call" | custom-call | tf_op jit(solution)/shard_map/pallas_call | solution.py:94
  22.3 17.7 %shard_map.51 = f32[256,2048]{1,0:T(8,128)} custom-call(s32[8,8]{1,0:T(8,128)} %mask_ref.3, bf16[2048,2048]{1,0:T(8,128)(2,1)} %g_ref.3, bf16[256,2048]{1,0:T(8,128)(2,1)} %bitcast.10), custom_call_target="tpu_custom_call" | custom-call | tf_op jit(solution)/shard_map/pallas_call | solution.py:139
  40.0 55.8 %shard_map.52 = f32[16,2048]{1,0:T(8,128)} custom-call(f32[16,16,2048]{2,1,0:T(8,128)} %bitcast.7), custom_call_target="tpu_custom_call" | custom-call | tf_op jit(solution)/shard_map/pallas_call | solution.py:78
  95.9 1.5 convert_element_type.3.x_ref
  97.4 33.4 %shard_map.53 = bf16[16,16,2048]{2,1,0:T(8,128)(2,1)} custom-call(bf16[16,2048]{1,0:T(8,128)(2,1)} %convert_element_type.3.x_ref), custom_call_target="tpu_custom_call" | custom-call | tf_op jit(solution)/shard_map/pallas_call | solution.py:94
  130.8 15.4 %shard_map.54 = f32[256,2048]{1,0:T(8,128)} custom-call(s32[8,8]{1,0:T(8,128)} %mask_ref.3, bf16[256,2048]{1,0:T(8,128)(2,1)} %bitcast.9, bf16[2048,2048]{1,0:T(8,128)(2,1)} %g_ref.3), custom_call_target="tpu_custom_call" | custom-call | tf_op jit(solution)/shard_map/pallas_call | solution.py:158
  146.2 0.0 copy-start
  146.2 41.7 %shard_map.55 = f32[16,2048]{1,0:T(8,128)} custom-call(f32[16,16,2048]{2,1,0:T(8,128)} %bitcast.8), custom_call_target="tpu_custom_call" | custom-call | tf_op jit(solution)/shard_map/pallas_call | solution.py:78
  187.9 0.0 copy-done
  188.0 0.7 copy.7
  188.6 1.6 copy.8
Async XLA Ops:
  146.2 41.8 %copy-start = (f32[16,2048]{1,0:T(8,128)S(1)}, f32[16,2048]{1,0:T(8,128)}, u32[]{:S(2)}) copy-start(f32[16,2048]{1,0:T(8,128)} %shard_map.52) | copy-start | bytes 393220

commit v4 on v3

--- a/solution.py
+++ b/solution.py
@@ -105,31 +105,29 @@
     )(x)
 
 
+def _mask_lanes(mask_ref, nb, bs, width, row=None, col=None):
+    blk = lax.broadcasted_iota(jnp.int32, (1, width), 1) // bs
+    keep = jnp.zeros((1, width), jnp.int32)
+    for b in range(nb):
+        value = mask_ref[row, b] if col is None else mask_ref[b, col]
+        keep = jnp.where(blk == b, value, keep)
+    return keep != 0
+
+
 def _sketch_kernel(nb, bs, mask_ref, g_ref, p_ref, o_ref):
     i = pl.program_id(0)
-    o_ref[...] = jnp.zeros_like(o_ref)
-    for j in range(nb):
-        @pl.when(mask_ref[i, j] != 0)
-        def _():
-            o_ref[...] += lax.dot_general(
-                p_ref[:, j * bs:(j + 1) * bs],
-                g_ref[:, j * bs:(j + 1) * bs],
-                (((1,), (1,)), ((), ())),
-                preferred_element_type=jnp.float32,
-            )
+    keep = _mask_lanes(mask_ref, nb, bs, p_ref.shape[1], row=i)
+    p = jnp.where(keep, p_ref[...], jnp.zeros_like(p_ref))
+    o_ref[...] = lax.dot_general(
+        p, g_ref[...], (((1,), (1,)), ((), ())), preferred_element_type=jnp.float32
+    )
 
 
 def _adjoint_kernel(nb, bs, mask_ref, l_ref, g_ref, o_ref):
     j = pl.program_id(0)
-    o_ref[...] = jnp.zeros_like(o_ref)
-    for i in range(nb):
-        @pl.when(mask_ref[i, j] != 0)
-        def _():
-            o_ref[...] += jnp.dot(
-                l_ref[:, i * bs:(i + 1) * bs],
-                g_ref[i * bs:(i + 1) * bs, :],
-                preferred_element_type=jnp.float32,
-            )
+    keep = _mask_lanes(mask_ref, nb, bs, l_ref.shape[1], col=j)
+    lowered = jnp.where(keep, l_ref[...], jnp.zeros_like(l_ref))
+    o_ref[...] = jnp.dot(lowered, g_ref[...], preferred_element_type=jnp.float32)
 
 
 def _sketch_partial(mask, green, probes_t):

time: 191 us -> 177 us (0.927)
  Pallas kernels: 186 us -> 172 us
    pallas_call x1, Pallas kernels: 17.7 us -> 9.8 us  [_sketch_partial(): pl.pallas_call(functools.partial(_sketch_kernel, cb, bs), out_shape=jax.S...]
    pallas_call x1, Pallas kernels: 15.4 us -> 9.68 us  [_adjoint_partial(): pl.pallas_call(functools.partial(_adjoint_kernel, rb, bs), out_shape=jax....]
where the time goes in v4:
time: 177 us
  Pallas kernels  172 us (97%)
  local copies, waits for them, and re-layouts  2.23 us (1%)
    pallas_call x2, Pallas kernels, _reduce_scatter(): pl.pallas_call(functools.partial(_rs_kernel, axis, other_axis, n), out_sh...  98.6 us
    pallas_call x2, Pallas kernels, _all_gather(): pl.pallas_call(functools.partial(_ag_kernel, axis, other_axis, n), out_sh...  54.3 us
    pallas_call x1, Pallas kernels, _sketch_partial(): pl.pallas_call(functools.partial(_sketch_kernel, cb, bs), out_shape=jax.S...  9.8 us
    pallas_call x1, Pallas kernels, _adjoint_partial(): pl.pallas_call(functools.partial(_adjoint_kernel, rb, bs), out_shape=jax....  9.68 us

profile of v4, /device:TPU:93, one launch (start us, length us, event | category | flops | bytes accessed | tf_op | source)
XLA Modules:
  0.0 176.8 jit_solution(2706750792600974534)
XLA Ops:
  0.6 21.7 %shard_map.50 = bf16[16,16,2048]{2,1,0:T(8,128)(2,1)} custom-call(bf16[16,2048]{1,0:T(8,128)(2,1)} %bitcast.13), custom_call_target="tpu_custom_call" | custom-call | tf_op jit(solution)/shard_map/pallas_call | solution.py:94
  22.3 9.8 %shard_map.51 = f32[256,2048]{1,0:T(8,128)} custom-call(s32[8,8]{1,0:T(8,128)} %mask_ref.3, bf16[2048,2048]{1,0:T(8,128)(2,1)} %g_ref.3, bf16[256,2048]{1,0:T(8,128)(2,1)} %bitcast.10), custom_call_target="tpu_custom_call" | custom-call | tf_op jit(solution)/shard_map/pallas_call | solution.py:137
  32.1 59.4 %shard_map.52 = f32[16,2048]{1,0:T(8,128)} custom-call(f32[16,16,2048]{2,1,0:T(8,128)} %bitcast.7), custom_call_target="tpu_custom_call" | custom-call | tf_op jit(solution)/shard_map/pallas_call | solution.py:78
  91.6 1.5 convert_element_type.3.x_ref
  93.1 32.6 %shard_map.53 = bf16[16,16,2048]{2,1,0:T(8,128)(2,1)} custom-call(bf16[16,2048]{1,0:T(8,128)(2,1)} %convert_element_type.3.x_ref), custom_call_target="tpu_custom_call" | custom-call | tf_op jit(solution)/shard_map/pallas_call | solution.py:94
  125.7 9.7 %shard_map.54 = f32[256,2048]{1,0:T(8,128)} custom-call(s32[8,8]{1,0:T(8,128)} %mask_ref.3, bf16[256,2048]{1,0:T(8,128)(2,1)} %bitcast.9, bf16[2048,2048]{1,0:T(8,128)(2,1)} %g_ref.3), custom_call_target="tpu_custom_call" | custom-call | tf_op jit(solution)/shard_map/pallas_call | solution.py:156
  135.4 0.0 copy-start
  135.4 39.2 %shard_map.55 = f32[16,2048]{1,0:T(8,128)} custom-call(f32[16,16,2048]{2,1,0:T(8,128)} %bitcast.8), custom_call_target="tpu_custom_call" | custom-call | tf_op jit(solution)/shard_map/pallas_call | solution.py:78
  174.6 0.0 copy-done
  174.6 0.7 copy.7
  175.2 1.6 copy.8
Async XLA Ops:
  135.4 39.2 %copy-start = (f32[16,2048]{1,0:T(8,128)S(1)}, f32[16,2048]{1,0:T(8,128)}, u32[]{:S(2)}) copy-start(f32[16,2048]{1,0:T(8,128)} %shard_map.52) | copy-start | bytes 393220

commit v5 on v4

--- a/solution.py
+++ b/solution.py
@@ -71,6 +71,140 @@
         o_ref[lax.rem(me + n - 1 - d, n)] = recv[d]
     for copy in copies:
         copy.wait_send()
+
+
+def _row_greet(me, other, chips):
+    chip, core = me // 2, lax.rem(me, 2)
+    barrier = pltpu.get_barrier_semaphore()
+    pl.semaphore_signal(barrier, 1, device_id=(chip * 2 + 1 - core, other), device_id_type=MESH)
+    for d in range(1, chips):
+        peer = lax.rem(chip + d, chips) * 2 + core
+        pl.semaphore_signal(barrier, 1, device_id=(peer, other), device_id_type=MESH)
+    pl.semaphore_wait(barrier, chips)
+    return chip, core
+
+
+def _row_rs_kernel(chips, x_ref, o_ref, recv1, mid, recv2, s1, r1, s2, r2):
+    me = lax.axis_index("row")
+    other = lax.axis_index("col")
+    chip, core = _row_greet(me, other, chips)
+    sib = (chip * 2 + 1 - core, other)
+    first = []
+    for q in range(chips):
+        copy = pltpu.make_async_remote_copy(
+            src_ref=x_ref.at[q, 1 - core],
+            dst_ref=recv1.at[q],
+            send_sem=s1.at[q],
+            recv_sem=r1.at[q],
+            device_id=sib,
+            device_id_type=MESH,
+        )
+        copy.start()
+        first.append(copy)
+    for q in range(chips):
+        first[q].wait_recv()
+    for d in range(1, chips):
+        target = lax.rem(chip + d, chips)
+        mid[d - 1] = x_ref[target, core] + recv1[target]
+    sends = []
+    for d in range(1, chips):
+        target = lax.rem(chip + d, chips)
+        copy = pltpu.make_async_remote_copy(
+            src_ref=mid.at[d - 1],
+            dst_ref=recv2.at[d - 1],
+            send_sem=s2.at[d - 1],
+            recv_sem=r2.at[d - 1],
+            device_id=(target * 2 + core, other),
+            device_id_type=MESH,
+        )
+        copy.start()
+        sends.append(copy)
+    acc = x_ref[chip, core] + recv1[chip]
+    for d, copy in enumerate(sends):
+        copy.wait_recv()
+        acc = acc + recv2[d]
+    for copy in first + sends:
+        copy.wait_send()
+    o_ref[...] = acc
+
+
+def _row_ag_kernel(chips, x_ref, o_ref, recv_s, recv_a, recv_f, s1, r1, s2, r2):
+    me = lax.axis_index("row")
+    other = lax.axis_index("col")
+    chip, core = _row_greet(me, other, chips)
+    sib = (chip * 2 + 1 - core, other)
+    to_sib = pltpu.make_async_remote_copy(
+        src_ref=x_ref, dst_ref=recv_s, send_sem=s1.at[0], recv_sem=r1.at[0],
+        device_id=sib, device_id_type=MESH,
+    )
+    to_sib.start()
+    first = [to_sib]
+    for d in range(1, chips):
+        peer = lax.rem(chip + d, chips) * 2 + core
+        copy = pltpu.make_async_remote_copy(
+            src_ref=x_ref, dst_ref=recv_a.at[d - 1], send_sem=s1.at[d], recv_sem=r1.at[d],
+            device_id=(peer, other), device_id_type=MESH,
+        )
+        copy.start()
+        first.append(copy)
+    o_ref[chip, core] = x_ref[...]
+    forwards = []
+    for d in range(1, chips):
+        first[d].wait_recv()
+        copy = pltpu.make_async_remote_copy(
+            src_ref=recv_a.at[d - 1], dst_ref=recv_f.at[d - 1], send_sem=s2.at[d - 1],
+            recv_sem=r2.at[d - 1], device_id=sib, device_id_type=MESH,
+        )
+        copy.start()
+        forwards.append(copy)
+        o_ref[lax.rem(chip + chips - d, chips), core] = recv_a[d - 1]
+    to_sib.wait_recv()
+    o_ref[chip, 1 - core] = recv_s[...]
+    for d, copy in enumerate(forwards):
+        copy.wait_recv()
+        o_ref[lax.rem(chip + chips - 1 - d, chips), 1 - core] = recv_f[d]
+    for copy in first + forwards:
+        copy.wait_send()
+
+
+def _row_reduce_scatter(x, collective_id):
+    chips, _, rows, width = x.shape
+    return pl.pallas_call(
+        functools.partial(_row_rs_kernel, chips),
+        out_shape=jax.ShapeDtypeStruct((rows, width), x.dtype),
+        in_specs=[pl.BlockSpec(memory_space=pltpu.VMEM)],
+        out_specs=pl.BlockSpec(memory_space=pltpu.VMEM),
+        scratch_shapes=[
+            pltpu.VMEM((chips, rows, width), x.dtype),
+            pltpu.VMEM((chips - 1, rows, width), x.dtype),
+            pltpu.VMEM((chips - 1, rows, width), x.dtype),
+            pltpu.SemaphoreType.DMA((chips,)),
+            pltpu.SemaphoreType.DMA((chips,)),
+            pltpu.SemaphoreType.DMA((chips - 1,)),
+            pltpu.SemaphoreType.DMA((chips - 1,)),
+        ],
+        compiler_params=pltpu.CompilerParams(collective_id=collective_id, has_side_effects=True),
+    )(x)
+
+
+def _row_all_gather(x, chips, collective_id):
+    rows, width = x.shape
+    return pl.pallas_call(
+        functools.partial(_row_ag_kernel, chips),
+        out_shape=jax.ShapeDtypeStruct((chips, 2, rows, width), x.dtype),
+        in_specs=[pl.BlockSpec(memory_space=pltpu.VMEM)],
+        out_specs=pl.BlockSpec(memory_space=pltpu.VMEM),
+        scratch_shapes=[
+            pltpu.VMEM((rows, width), x.dtype),
+            pltpu.VMEM((chips - 1, rows, width), x.dtype),
+            pltpu.VMEM((chips - 1, rows, width), x.dtype),
+            pltpu.SemaphoreType.DMA((chips,)),
+            pltpu.SemaphoreType.DMA((chips,)),
+            pltpu.SemaphoreType.DMA((chips - 1,)),
+            pltpu.SemaphoreType.DMA((chips - 1,)),
+        ],
+        compiler_params=pltpu.CompilerParams(collective_id=collective_id, has_side_effects=True),
+    )(x)
 
 
 def _reduce_scatter(x, axis, other_axis, collective_id):
@@ -171,14 +305,14 @@
 def local(green, mask, probes):
     n_row = lax.axis_size("row")
     n_col = lax.axis_size("col")
-    probes_t = _all_gather(probes.T, "row", "col", n_row, 3)
-    k = probes_t.shape[0] * probes_t.shape[1]
+    probes_t = _row_all_gather(probes.T, n_row // 2, 3)
+    k = n_row * probes_t.shape[2]
     probes_t = probes_t.reshape(k, -1)
     partial_t = _sketch_partial(mask, green, probes_t)
     sketch_t = _reduce_scatter(partial_t.reshape(n_col, k // n_col, -1), "col", "row", 0)
     lowered_t = _all_gather(sketch_t.astype(jnp.bfloat16), "col", "row", n_col, 1).reshape(k, -1)
     term_t = _adjoint_partial(mask, lowered_t, green)
-    adjoint_t = _reduce_scatter(term_t.reshape(n_row, k // n_row, -1), "row", "col", 2)
+    adjoint_t = _row_reduce_scatter(term_t.reshape(n_row // 2, 2, k // n_row, -1), 2)
     return (sketch_t.T, adjoint_t.T)
 
 

time: 177 us -> 155 us (0.88); the launches traced: 177 us -> 153 us
  Pallas kernels: 172 us -> 148 us
    pallas_call x2 -> x1, Pallas kernels: 98.6 us -> 58.9 us  [_reduce_scatter(): pl.pallas_call(functools.partial(_rs_kernel, axis, other_axis, n), out_sh...]
    pallas_call x0 -> x2, Pallas kernels: none -> 38 us  [the longest x1 23.2 us: _row_reduce_scatter(): pl.pallas_call(functools.partial(_row_rs_kernel, chips), out_shape=jax.Sh...]
    pallas_call x2 -> x1, Pallas kernels: 54.3 us -> 31.9 us  [_all_gather(): pl.pallas_call(functools.partial(_ag_kernel, axis, other_axis, n), out_sh...]
where the time goes in v5:
time: 155 us; the launch traced here: 153 us
  Pallas kernels  148 us (95%)
  local copies, waits for them, and re-layouts  2.23 us (1%)
    pallas_call x1, Pallas kernels, _reduce_scatter(): pl.pallas_call(functools.partial(_rs_kernel, axis, other_axis, n), out_sh...  58.9 us
    pallas_call x1, Pallas kernels, _all_gather(): pl.pallas_call(functools.partial(_ag_kernel, axis, other_axis, n), out_sh...  31.9 us
    pallas_call x1, Pallas kernels, _row_reduce_scatter(): pl.pallas_call(functools.partial(_row_rs_kernel, chips), out_shape=jax.Sh...  23.2 us
    pallas_call x1, Pallas kernels, _row_all_gather(): pl.pallas_call(functools.partial(_row_ag_kernel, chips), out_shape=jax.Sh...  14.8 us
    pallas_call x1, Pallas kernels, _sketch_partial(): pl.pallas_call(functools.partial(_sketch_kernel, cb, bs), out_shape=jax.S...  9.81 us
    pallas_call x1, Pallas kernels, _adjoint_partial(): pl.pallas_call(functools.partial(_adjoint_kernel, rb, bs), out_shape=jax....  9.68 us

profile of v5, /device:TPU:93, one launch (start us, length us, event | category | flops | bytes accessed | tf_op | source)
XLA Modules:
  0.0 152.8 jit_solution(14930727594127220240)
XLA Ops:
  0.6 14.8 %shard_map.50 = bf16[8,2,16,2048]{3,2,1,0:T(8,128)(2,1)} custom-call(bf16[16,2048]{1,0:T(8,128)(2,1)} %bitcast.13), custom_call_target="tpu_custom_call" | custom-call | tf_op jit(solution)/shard_map/pallas_call | solution.py:192
  15.5 9.8 %shard_map.51 = f32[256,2048]{1,0:T(8,128)} custom-call(s32[8,8]{1,0:T(8,128)} %mask_ref.3, bf16[2048,2048]{1,0:T(8,128)(2,1)} %g_ref.3, bf16[256,2048]{1,0:T(8,128)(2,1)} %bitcast.10), custom_call_target="tpu_custom_call" | custom-call | tf_op jit(solution)/shard_map/pallas_call | solution.py:271
  25.3 58.9 %shard_map.52 = f32[16,2048]{1,0:T(8,128)} custom-call(f32[16,16,2048]{2,1,0:T(8,128)} %bitcast.7), custom_call_target="tpu_custom_call" | custom-call | tf_op jit(solution)/shard_map/pallas_call | solution.py:212
  84.2 1.5 %convert_element_type.3.x_ref = bf16[16,2048]{1,0:T(8,128)(2,1)} convert(f32[16,2048]{1,0:T(8,128)} %shard_map.52) | non-fusion elementwise | flops 32768 | bytes 196608 | tf_op jit(solution)/shard_map/convert_element_type | solution.py:313
  85.7 31.9 %shard_map.53 = bf16[16,16,2048]{2,1,0:T(8,128)(2,1)} custom-call(bf16[16,2048]{1,0:T(8,128)(2,1)} %convert_element_type.3.x_ref), custom_call_target="tpu_custom_call" | custom-call | tf_op jit(solution)/shard_map/pallas_call | solution.py:228
  117.7 9.7 %shard_map.54 = f32[256,2048]{1,0:T(8,128)} custom-call(s32[8,8]{1,0:T(8,128)} %mask_ref.3, bf16[256,2048]{1,0:T(8,128)(2,1)} %bitcast.9, bf16[2048,2048]{1,0:T(8,128)(2,1)} %g_ref.3), custom_call_target="tpu_custom_call" | custom-call | tf_op jit(solution)/shard_map/pallas_call | solution.py:290
  127.3 0.0 copy-start
  127.3 23.2 %shard_map.55 = f32[16,2048]{1,0:T(8,128)} custom-call(f32[8,2,16,2048]{3,2,1,0:T(8,128)} %bitcast.8), custom_call_target="tpu_custom_call" | custom-call | tf_op jit(solution)/shard_map/pallas_call | solution.py:172
  150.6 0.0 copy-done
  150.6 0.7 copy.7
  151.2 1.6 %copy.8 = f32[2048,16]{0,1:T(8,128)} copy(f32[2048,16]{0,1:T(8,128)} %bitcast.12) | data formatting | bytes 262144
Async XLA Ops:
  127.3 23.2 %copy-start = (f32[16,2048]{1,0:T(8,128)S(1)}, f32[16,2048]{1,0:T(8,128)}, u32[]{:S(2)}) copy-start(f32[16,2048]{1,0:T(8,128)} %shard_map.52) | copy-start | bytes 393220

commit v6 on v5

--- a/solution.py
+++ b/solution.py
@@ -73,22 +73,22 @@
         copy.wait_send()
 
 
-def _row_greet(me, other, chips):
+def _row_greet(axis, me, other, chips):
     chip, core = me // 2, lax.rem(me, 2)
     barrier = pltpu.get_barrier_semaphore()
-    pl.semaphore_signal(barrier, 1, device_id=(chip * 2 + 1 - core, other), device_id_type=MESH)
+    pl.semaphore_signal(barrier, 1, device_id=_peer(axis, other, chip * 2 + 1 - core), device_id_type=MESH)
     for d in range(1, chips):
         peer = lax.rem(chip + d, chips) * 2 + core
-        pl.semaphore_signal(barrier, 1, device_id=(peer, other), device_id_type=MESH)
+        pl.semaphore_signal(barrier, 1, device_id=_peer(axis, other, peer), device_id_type=MESH)
     pl.semaphore_wait(barrier, chips)
     return chip, core
 
 
-def _row_rs_kernel(chips, x_ref, o_ref, recv1, mid, recv2, s1, r1, s2, r2):
-    me = lax.axis_index("row")
-    other = lax.axis_index("col")
-    chip, core = _row_greet(me, other, chips)
-    sib = (chip * 2 + 1 - core, other)
+def _row_rs_kernel(axis, other_axis, chips, x_ref, o_ref, recv1, mid, recv2, s1, r1, s2, r2):
+    me = lax.axis_index(axis)
+    other = lax.axis_index(other_axis)
+    chip, core = _row_greet(axis, me, other, chips)
+    sib = _peer(axis, other, chip * 2 + 1 - core)
     first = []
     for q in range(chips):
         copy = pltpu.make_async_remote_copy(
@@ -114,7 +114,7 @@
             dst_ref=recv2.at[d - 1],
             send_sem=s2.at[d - 1],
             recv_sem=r2.at[d - 1],
-            device_id=(target * 2 + core, other),
+            device_id=_peer(axis, other, target * 2 + core),
             device_id_type=MESH,
         )
         copy.start()
@@ -128,11 +128,11 @@
     o_ref[...] = acc
 
 
-def _row_ag_kernel(chips, x_ref, o_ref, recv_s, recv_a, recv_f, s1, r1, s2, r2):
-    me = lax.axis_index("row")
-    other = lax.axis_index("col")
-    chip, core = _row_greet(me, other, chips)
-    sib = (chip * 2 + 1 - core, other)
+def _row_ag_kernel(axis, other_axis, chips, x_ref, o_ref, recv_s, recv_a, recv_f, s1, r1, s2, r2):
+    me = lax.axis_index(axis)
+    other = lax.axis_index(other_axis)
+    chip, core = _row_greet(axis, me, other, chips)
+    sib = _peer(axis, other, chip * 2 + 1 - core)
     to_sib = pltpu.make_async_remote_copy(
         src_ref=x_ref, dst_ref=recv_s, send_sem=s1.at[0], recv_sem=r1.at[0],
         device_id=sib, device_id_type=MESH,
@@ -143,7 +143,7 @@
         peer = lax.rem(chip + d, chips) * 2 + core
         copy = pltpu.make_async_remote_copy(
             src_ref=x_ref, dst_ref=recv_a.at[d - 1], send_sem=s1.at[d], recv_sem=r1.at[d],
-            device_id=(peer, other), device_id_type=MESH,
+            device_id=_peer(axis, other, peer), device_id_type=MESH,
         )
         copy.start()
         first.append(copy)
@@ -167,10 +167,10 @@
         copy.wait_send()
 
 
-def _row_reduce_scatter(x, collective_id):
+def _row_reduce_scatter(x, axis, other_axis, collective_id):
     chips, _, rows, width = x.shape
     return pl.pallas_call(
-        functools.partial(_row_rs_kernel, chips),
+        functools.partial(_row_rs_kernel, axis, other_axis, chips),
         out_shape=jax.ShapeDtypeStruct((rows, width), x.dtype),
         in_specs=[pl.BlockSpec(memory_space=pltpu.VMEM)],
         out_specs=pl.BlockSpec(memory_space=pltpu.VMEM),
@@ -187,10 +187,10 @@
     )(x)
 
 
-def _row_all_gather(x, chips, collective_id):
+def _row_all_gather(x, axis, other_axis, chips, collective_id):
     rows, width = x.shape
     return pl.pallas_call(
-        functools.partial(_row_ag_kernel, chips),
+        functools.partial(_row_ag_kernel, axis, other_axis, chips),
         out_shape=jax.ShapeDtypeStruct((chips, 2, rows, width), x.dtype),
         in_specs=[pl.BlockSpec(memory_space=pltpu.VMEM)],
         out_specs=pl.BlockSpec(memory_space=pltpu.VMEM),
@@ -305,14 +305,14 @@
 def local(green, mask, probes):
     n_row = lax.axis_size("row")
     n_col = lax.axis_size("col")
-    probes_t = _row_all_gather(probes.T, n_row // 2, 3)
+    probes_t = _row_all_gather(probes.T, "row", "col", n_row // 2, 3)
     k = n_row * probes_t.shape[2]
     probes_t = probes_t.reshape(k, -1)
     partial_t = _sketch_partial(mask, green, probes_t)
-    sketch_t = _reduce_scatter(partial_t.reshape(n_col, k // n_col, -1), "col", "row", 0)
-    lowered_t = _all_gather(sketch_t.astype(jnp.bfloat16), "col", "row", n_col, 1).reshape(k, -1)
+    sketch_t = _row_reduce_scatter(partial_t.reshape(n_col // 2, 2, k // n_col, -1), "col", "row", 0)
+    lowered_t = _row_all_gather(sketch_t.astype(jnp.bfloat16), "col", "row", n_col // 2, 1).reshape(k, -1)
     term_t = _adjoint_partial(mask, lowered_t, green)
-    adjoint_t = _row_reduce_scatter(term_t.reshape(n_row // 2, 2, k // n_row, -1), 2)
+    adjoint_t = _row_reduce_scatter(term_t.reshape(n_row // 2, 2, k // n_row, -1), "row", "col", 2)
     return (sketch_t.T, adjoint_t.T)
 
 

time: 155 us -> 146 us (0.942)
  Pallas kernels: 148 us -> 139 us
    pallas_call x4, Pallas kernels: 129 us -> 119 us  [the longest x2 78.7 us: _row_reduce_scatter(): pl.pallas_call(functools.partial(_row_rs_kernel, axis, other_axis, chips)...]
where the time goes in v6:
time: 146 us; the launch traced here: 143 us
  Pallas kernels  139 us (95%)
  local copies, waits for them, and re-layouts  2.23 us (2%)
  other arithmetic  1.54 us (1%)
    pallas_call x2, Pallas kernels, _row_reduce_scatter(): pl.pallas_call(functools.partial(_row_rs_kernel, axis, other_axis, chips)...  78.7 us
    pallas_call x2, Pallas kernels, _row_all_gather(): pl.pallas_call(functools.partial(_row_ag_kernel, axis, other_axis, chips)...  40.5 us
    pallas_call x1, Pallas kernels, _sketch_partial(): pl.pallas_call(functools.partial(_sketch_kernel, cb, bs), out_shape=jax.S...  9.81 us
    pallas_call x1, Pallas kernels, _adjoint_partial(): pl.pallas_call(functools.partial(_adjoint_kernel, rb, bs), out_shape=jax....  9.68 us

profile of v6, /device:TPU:93, one launch (start us, length us, event | category | flops | bytes accessed | tf_op | source)
XLA Modules:
  0.0 143.2 jit_solution(10847331418391188173)
XLA Ops:
  0.6 14.8 %shard_map.50 = bf16[8,2,16,2048]{3,2,1,0:T(8,128)(2,1)} custom-call(bf16[16,2048]{1,0:T(8,128)(2,1)} %bitcast.13), custom_call_target="tpu_custom_call" | custom-call | tf_op jit(solution)/shard_map/pallas_call | solution.py:192
  15.5 9.8 %shard_map.51 = f32[256,2048]{1,0:T(8,128)} custom-call(s32[8,8]{1,0:T(8,128)} %mask_ref.3, bf16[2048,2048]{1,0:T(8,128)(2,1)} %g_ref.3, bf16[256,2048]{1,0:T(8,128)(2,1)} %bitcast.10), custom_call_target="tpu_custom_call" | custom-call | tf_op jit(solution)/shard_map/pallas_call | solution.py:271
  25.3 55.8 %shard_map.52 = f32[16,2048]{1,0:T(8,128)} custom-call(f32[8,2,16,2048]{3,2,1,0:T(8,128)} %bitcast.7), custom_call_target="tpu_custom_call" | custom-call | tf_op jit(solution)/shard_map/pallas_call | solution.py:172
  81.1 1.5 %convert_element_type.3.x_ref = bf16[16,2048]{1,0:T(8,128)(2,1)} convert(f32[16,2048]{1,0:T(8,128)} %shard_map.52) | non-fusion elementwise | flops 32768 | bytes 196608 | tf_op jit(solution)/shard_map/convert_element_type | solution.py:313
  82.6 25.7 %shard_map.53 = bf16[8,2,16,2048]{3,2,1,0:T(8,128)(2,1)} custom-call(bf16[16,2048]{1,0:T(8,128)(2,1)} %convert_element_type.3.x_ref), custom_call_target="tpu_custom_call" | custom-call | tf_op jit(solution)/shard_map/pallas_call | solution.py:192
  108.3 9.7 %shard_map.54 = f32[256,2048]{1,0:T(8,128)} custom-call(s32[8,8]{1,0:T(8,128)} %mask_ref.3, bf16[256,2048]{1,0:T(8,128)(2,1)} %bitcast.9, bf16[2048,2048]{1,0:T(8,128)(2,1)} %g_ref.3), custom_call_target="tpu_custom_call" | custom-call | tf_op jit(solution)/shard_map/pallas_call | solution.py:290
  118.0 0.0 copy-start
  118.0 22.9 %shard_map.55 = f32[16,2048]{1,0:T(8,128)} custom-call(f32[8,2,16,2048]{3,2,1,0:T(8,128)} %bitcast.8), custom_call_target="tpu_custom_call" | custom-call | tf_op jit(solution)/shard_map/pallas_call | solution.py:172
  141.0 0.0 copy-done
  141.0 0.7 copy.7
  141.6 1.6 %copy.8 = f32[2048,16]{0,1:T(8,128)} copy(f32[2048,16]{0,1:T(8,128)} %bitcast.12) | data formatting | bytes 262144
Async XLA Ops:
  118.0 22.9 %copy-start = (f32[16,2048]{1,0:T(8,128)S(1)}, f32[16,2048]{1,0:T(8,128)}, u32[]{:S(2)}) copy-start(f32[16,2048]{1,0:T(8,128)} %shard_map.52) | copy-start | bytes 393220

commit v7 on v6

--- a/solution.py
+++ b/solution.py
@@ -88,6 +88,10 @@
     me = lax.axis_index(axis)
     other = lax.axis_index(other_axis)
     chip, core = _row_greet(axis, me, other, chips)
+    _rs_body(axis, other, chips, chip, core, x_ref, o_ref, recv1, mid, recv2, s1, r1, s2, r2)
+
+
+def _rs_body(axis, other, chips, chip, core, x_ref, o_ref, recv1, mid, recv2, s1, r1, s2, r2):
     sib = _peer(axis, other, chip * 2 + 1 - core)
     first = []
     for q in range(chips):
@@ -132,6 +136,10 @@
     me = lax.axis_index(axis)
     other = lax.axis_index(other_axis)
     chip, core = _row_greet(axis, me, other, chips)
+    _ag_body(axis, other, chips, chip, core, x_ref, o_ref, recv_s, recv_a, recv_f, s1, r1, s2, r2)
+
+
+def _ag_body(axis, other, chips, chip, core, x_ref, o_ref, recv_s, recv_a, recv_f, s1, r1, s2, r2):
     sib = _peer(axis, other, chip * 2 + 1 - core)
     to_sib = pltpu.make_async_remote_copy(
         src_ref=x_ref, dst_ref=recv_s, send_sem=s1.at[0], recv_sem=r1.at[0],
@@ -165,6 +173,47 @@
         o_ref[lax.rem(chip + chips - 1 - d, chips), 1 - core] = recv_f[d]
     for copy in first + forwards:
         copy.wait_send()
+
+
+def _ar_kernel(axis, other_axis, chips, x_ref, o_ref, g_ref, low, *scratch):
+    me = lax.axis_index(axis)
+    other = lax.axis_index(other_axis)
+    chip, core = _row_greet(axis, me, other, chips)
+    _rs_body(axis, other, chips, chip, core, x_ref, o_ref, *scratch[:7])
+    low[...] = o_ref[...].astype(low.dtype)
+    _ag_body(axis, other, chips, chip, core, low, g_ref, *scratch[7:])
+
+
+def _all_reduce(x, axis, other_axis, collective_id):
+    chips, _, rows, width = x.shape
+    low = jnp.bfloat16
+    return pl.pallas_call(
+        functools.partial(_ar_kernel, axis, other_axis, chips),
+        out_shape=(
+            jax.ShapeDtypeStruct((rows, width), x.dtype),
+            jax.ShapeDtypeStruct((chips, 2, rows, width), low),
+        ),
+        in_specs=[pl.BlockSpec(memory_space=pltpu.VMEM)],
+        out_specs=(pl.BlockSpec(memory_space=pltpu.VMEM), pl.BlockSpec(memory_space=pltpu.VMEM)),
+        scratch_shapes=[
+            pltpu.VMEM((rows, width), low),
+            pltpu.VMEM((chips, rows, width), x.dtype),
+            pltpu.VMEM((chips - 1, rows, width), x.dtype),
+            pltpu.VMEM((chips - 1, rows, width), x.dtype),
+            pltpu.SemaphoreType.DMA((chips,)),
+            pltpu.SemaphoreType.DMA((chips,)),
+            pltpu.SemaphoreType.DMA((chips - 1,)),
+            pltpu.SemaphoreType.DMA((chips - 1,)),
+            pltpu.VMEM((rows, width), low),
+            pltpu.VMEM((chips - 1, rows, width), low),
+            pltpu.VMEM((chips - 1, rows, width), low),
+            pltpu.SemaphoreType.DMA((chips,)),
+            pltpu.SemaphoreType.DMA((chips,)),
+            pltpu.SemaphoreType.DMA((chips - 1,)),
+            pltpu.SemaphoreType.DMA((chips - 1,)),
+        ],
+        compiler_params=pltpu.CompilerParams(collective_id=collective_id, has_side_effects=True),
+    )(x)
 
 
 def _row_reduce_scatter(x, axis, other_axis, collective_id):
@@ -309,8 +358,8 @@
     k = n_row * probes_t.shape[2]
     probes_t = probes_t.reshape(k, -1)
     partial_t = _sketch_partial(mask, green, probes_t)
-    sketch_t = _row_reduce_scatter(partial_t.reshape(n_col // 2, 2, k // n_col, -1), "col", "row", 0)
-    lowered_t = _row_all_gather(sketch_t.astype(jnp.bfloat16), "col", "row", n_col // 2, 1).reshape(k, -1)
+    sketch_t, lowered_t = _all_reduce(partial_t.reshape(n_col // 2, 2, k // n_col, -1), "col", "row", 0)
+    lowered_t = lowered_t.reshape(k, -1)
     term_t = _adjoint_partial(mask, lowered_t, green)
     adjoint_t = _row_reduce_scatter(term_t.reshape(n_row // 2, 2, k // n_row, -1), "row", "col", 2)
     return (sketch_t.T, adjoint_t.T)

time: 146 us -> 142 us (0.973)
  the two profiles are of different devices: /device:TPU:93 before, /device:TPU:27 now
where the time goes in v7:
time: 142 us; the launch traced here: 141 us
  Pallas kernels  138 us (97%)
  local copies, waits for them, and re-layouts  2.23 us (2%)
    pallas_call x1, Pallas kernels, _all_reduce(): pl.pallas_call(functools.partial(_ar_kernel, axis, other_axis, chips), ou...  80.8 us
    pallas_call x1, Pallas kernels, _row_reduce_scatter(): pl.pallas_call(functools.partial(_row_rs_kernel, axis, other_axis, chips)...  23.3 us
    pallas_call x1, Pallas kernels, _row_all_gather(): pl.pallas_call(functools.partial(_row_ag_kernel, axis, other_axis, chips)...  14.8 us
    pallas_call x1, Pallas kernels, _sketch_partial(): pl.pallas_call(functools.partial(_sketch_kernel, cb, bs), out_shape=jax.S...  9.8 us
    pallas_call x1, Pallas kernels, _adjoint_partial(): pl.pallas_call(functools.partial(_adjoint_kernel, rb, bs), out_shape=jax....  9.69 us

profile of v7, /device:TPU:27, one launch (start us, length us, event | category | flops | bytes accessed | tf_op | source)
XLA Modules:
  0.0 141.2 jit_solution(5682987892339798212)
XLA Ops:
  0.6 14.8 %shard_map.50 = bf16[8,2,16,2048]{3,2,1,0:T(8,128)(2,1)} custom-call(bf16[16,2048]{1,0:T(8,128)(2,1)} %bitcast.13), custom_call_target="tpu_custom_call" | custom-call | tf_op jit(solution)/shard_map/pallas_call | solution.py:241
  15.4 9.8 %shard_map.51 = f32[256,2048]{1,0:T(8,128)} custom-call(s32[8,8]{1,0:T(8,128)} %mask_ref.3, bf16[2048,2048]{1,0:T(8,128)(2,1)} %g_ref.3, bf16[256,2048]{1,0:T(8,128)(2,1)} %bitcast.9), custom_call_target="tpu_custom_call" | custom-call | tf_op jit(solution)/shard_map/pallas_call | solution.py:320
  25.2 80.8 %shard_map.52 = (f32[16,2048]{1,0:T(8,128)}, bf16[8,2,16,2048]{3,2,1,0:T(8,128)(2,1)}) custom-call(f32[8,2,16,2048]{3,2,1,0:T(8,128)} %bitcast.7), custom_call_target="tpu_custom_call" | custom-call | tf_op jit(solution)/shard_map/pallas_call | solution.py:190
  106.0 9.7 %shard_map.53 = f32[256,2048]{1,0:T(8,128)} custom-call(s32[8,8]{1,0:T(8,128)} %mask_ref.3, bf16[256,2048]{1,0:T(8,128)(2,1)} %bitcast.10, bf16[2048,2048]{1,0:T(8,128)(2,1)} %g_ref.3), custom_call_target="tpu_custom_call" | custom-call | tf_op jit(solution)/shard_map/pallas_call | solution.py:339
  115.7 0.0 copy-start
  115.7 23.3 %shard_map.54 = f32[16,2048]{1,0:T(8,128)} custom-call(f32[8,2,16,2048]{3,2,1,0:T(8,128)} %bitcast.8), custom_call_target="tpu_custom_call" | custom-call | tf_op jit(solution)/shard_map/pallas_call | solution.py:221
  139.0 0.0 copy-done
  139.0 0.7 copy.7
  139.7 1.6 %copy.8 = f32[2048,16]{0,1:T(8,128)} copy(f32[2048,16]{0,1:T(8,128)} %bitcast.11) | data formatting | bytes 262144
Async XLA Ops:
  115.7 23.3 %copy-start = (f32[16,2048]{1,0:T(8,128)S(1)}, f32[16,2048]{1,0:T(8,128)}, u32[]{:S(2)}) copy-start(f32[16,2048]{1,0:T(8,128)} %get-tuple-element.4) | copy-start | bytes 393220

commit v8 on v7

--- a/solution.py
+++ b/solution.py
@@ -73,12 +73,24 @@
         copy.wait_send()
 
 
+def _split(axis, me):
+    if axis == "col":
+        return (me // 4) * 2 + lax.rem(me, 2), lax.rem(me // 2, 2)
+    return me // 2, lax.rem(me, 2)
+
+
+def _index(axis, group, bit):
+    if axis == "col":
+        return (group // 2) * 4 + bit * 2 + lax.rem(group, 2)
+    return group * 2 + bit
+
+
 def _row_greet(axis, me, other, chips):
-    chip, core = me // 2, lax.rem(me, 2)
+    chip, core = _split(axis, me)
     barrier = pltpu.get_barrier_semaphore()
-    pl.semaphore_signal(barrier, 1, device_id=_peer(axis, other, chip * 2 + 1 - core), device_id_type=MESH)
-    for d in range(1, chips):
-        peer = lax.rem(chip + d, chips) * 2 + core
+    pl.semaphore_signal(barrier, 1, device_id=_peer(axis, other, _index(axis, chip, 1 - core)), device_id_type=MESH)
+    for d in range(1, chips):
+        peer = _index(axis, lax.rem(chip + d, chips), core)
         pl.semaphore_signal(barrier, 1, device_id=_peer(axis, other, peer), device_id_type=MESH)
     pl.semaphore_wait(barrier, chips)
     return chip, core
@@ -92,11 +104,11 @@
 
 
 def _rs_body(axis, other, chips, chip, core, x_ref, o_ref, recv1, mid, recv2, s1, r1, s2, r2):
-    sib = _peer(axis, other, chip * 2 + 1 - core)
+    sib = _peer(axis, other, _index(axis, chip, 1 - core))
     first = []
     for q in range(chips):
         copy = pltpu.make_async_remote_copy(
-            src_ref=x_ref.at[q, 1 - core],
+            src_ref=x_ref.at[_index(axis, q, 1 - core)],
             dst_ref=recv1.at[q],
             send_sem=s1.at[q],
             recv_sem=r1.at[q],
@@ -109,7 +121,7 @@
         first[q].wait_recv()
     for d in range(1, chips):
         target = lax.rem(chip + d, chips)
-        mid[d - 1] = x_ref[target, core] + recv1[target]
+        mid[d - 1] = x_ref[_index(axis, target, core)] + recv1[target]
     sends = []
     for d in range(1, chips):
         target = lax.rem(chip + d, chips)
@@ -118,12 +130,12 @@
             dst_ref=recv2.at[d - 1],
             send_sem=s2.at[d - 1],
             recv_sem=r2.at[d - 1],
-            device_id=_peer(axis, other, target * 2 + core),
+            device_id=_peer(axis, other, _index(axis, target, core)),
             device_id_type=MESH,
         )
         copy.start()
         sends.append(copy)
-    acc = x_ref[chip, core] + recv1[chip]
+    acc = x_ref[_index(axis, chip, core)] + recv1[chip]
     for d, copy in enumerate(sends):
         copy.wait_recv()
         acc = acc + recv2[d]
@@ -140,7 +152,7 @@
 
 
 def _ag_body(axis, other, chips, chip, core, x_ref, o_ref, recv_s, recv_a, recv_f, s1, r1, s2, r2):
-    sib = _peer(axis, other, chip * 2 + 1 - core)
+    sib = _peer(axis, other, _index(axis, chip, 1 - core))
     to_sib = pltpu.make_async_remote_copy(
         src_ref=x_ref, dst_ref=recv_s, send_sem=s1.at[0], recv_sem=r1.at[0],
         device_id=sib, device_id_type=MESH,
@@ -148,14 +160,14 @@
     to_sib.start()
     first = [to_sib]
     for d in range(1, chips):
-        peer = lax.rem(chip + d, chips) * 2 + core
+        peer = _index(axis, lax.rem(chip + d, chips), core)
         copy = pltpu.make_async_remote_copy(
             src_ref=x_ref, dst_ref=recv_a.at[d - 1], send_sem=s1.at[d], recv_sem=r1.at[d],
             device_id=_peer(axis, other, peer), device_id_type=MESH,
         )
         copy.start()
         first.append(copy)
-    o_ref[chip, core] = x_ref[...]
+    o_ref[_index(axis, chip, core)] = x_ref[...]
     forwards = []
     for d in range(1, chips):
         first[d].wait_recv()
@@ -165,12 +177,12 @@
         )
         copy.start()
         forwards.append(copy)
-        o_ref[lax.rem(chip + chips - d, chips), core] = recv_a[d - 1]
+        o_ref[_index(axis, lax.rem(chip + chips - d, chips), core)] = recv_a[d - 1]
     to_sib.wait_recv()
-    o_ref[chip, 1 - core] = recv_s[...]
+    o_ref[_index(axis, chip, 1 - core)] = recv_s[...]
     for d, copy in enumerate(forwards):
         copy.wait_recv()
-        o_ref[lax.rem(chip + chips - 1 - d, chips), 1 - core] = recv_f[d]
+        o_ref[_index(axis, lax.rem(chip + chips - 1 - d, chips), 1 - core)] = recv_f[d]
     for copy in first + forwards:
         copy.wait_send()
 
@@ -185,13 +197,14 @@
 
 
 def _all_reduce(x, axis, other_axis, collective_id):
-    chips, _, rows, width = x.shape
+    n, rows, width = x.shape
+    chips = n // 2
     low = jnp.bfloat16
     return pl.pallas_call(
         functools.partial(_ar_kernel, axis, other_axis, chips),
         out_shape=(
             jax.ShapeDtypeStruct((rows, width), x.dtype),
-            jax.ShapeDtypeStruct((chips, 2, rows, width), low),
+            jax.ShapeDtypeStruct((n, rows, width), low),
         ),
         in_specs=[pl.BlockSpec(memory_space=pltpu.VMEM)],
         out_specs=(pl.BlockSpec(memory_space=pltpu.VMEM), pl.BlockSpec(memory_space=pltpu.VMEM)),
@@ -217,7 +230,8 @@
 
 
 def _row_reduce_scatter(x, axis, other_axis, collective_id):
-    chips, _, rows, width = x.shape
+    n, rows, width = x.shape
+    chips = n // 2
     return pl.pallas_call(
         functools.partial(_row_rs_kernel, axis, other_axis, chips),
         out_shape=jax.ShapeDtypeStruct((rows, width), x.dtype),
@@ -240,7 +254,7 @@
     rows, width = x.shape
     return pl.pallas_call(
         functools.partial(_row_ag_kernel, axis, other_axis, chips),
-        out_shape=jax.ShapeDtypeStruct((chips, 2, rows, width), x.dtype),
+        out_shape=jax.ShapeDtypeStruct((2 * chips, rows, width), x.dtype),
         in_specs=[pl.BlockSpec(memory_space=pltpu.VMEM)],
         out_specs=pl.BlockSpec(memory_space=pltpu.VMEM),
         scratch_shapes=[
@@ -355,13 +369,13 @@
     n_row = lax.axis_size("row")
     n_col = lax.axis_size("col")
     probes_t = _row_all_gather(probes.T, "row", "col", n_row // 2, 3)
-    k = n_row * probes_t.shape[2]
+    k = n_row * probes_t.shape[1]
     probes_t = probes_t.reshape(k, -1)
     partial_t = _sketch_partial(mask, green, probes_t)
-    sketch_t, lowered_t = _all_reduce(partial_t.reshape(n_col // 2, 2, k // n_col, -1), "col", "row", 0)
+    sketch_t, lowered_t = _all_reduce(partial_t.reshape(n_col, k // n_col, -1), "col", "row", 0)
     lowered_t = lowered_t.reshape(k, -1)
     term_t = _adjoint_partial(mask, lowered_t, green)
-    adjoint_t = _row_reduce_scatter(term_t.reshape(n_row // 2, 2, k // n_row, -1), "row", "col", 2)
+    adjoint_t = _row_reduce_scatter(term_t.reshape(n_row, k // n_row, -1), "row", "col", 2)
     return (sketch_t.T, adjoint_t.T)
 
 

time: 142 us -> 148 us (1.042)
  the two profiles are of different devices: /device:TPU:27 before, /device:TPU:29 now
where the time goes in v8:
time: 148 us
  Pallas kernels  145 us (98%)
  local copies, waits for them, and re-layouts  2.23 us (2%)
    pallas_call x1, Pallas kernels, _all_reduce(): pl.pallas_call(functools.partial(_ar_kernel, axis, other_axis, chips), ou...  85.7 us
    pallas_call x1, Pallas kernels, _row_reduce_scatter(): pl.pallas_call(functools.partial(_row_rs_kernel, axis, other_axis, chips)...  25 us
    pallas_call x1, Pallas kernels, _row_all_gather(): pl.pallas_call(functools.partial(_row_ag_kernel, axis, other_axis, chips)...  14.8 us
    pallas_call x1, Pallas kernels, _sketch_partial(): pl.pallas_call(functools.partial(_sketch_kernel, cb, bs), out_shape=jax.S...  9.8 us
    pallas_call x1, Pallas kernels, _adjoint_partial(): pl.pallas_call(functools.partial(_adjoint_kernel, rb, bs), out_shape=jax....  9.69 us

profile of v8, /device:TPU:29, one launch (start us, length us, event | category | flops | bytes accessed | tf_op | source)
XLA Modules:
  0.0 147.8 jit_solution(3473014933819454000)
XLA Ops:
  0.6 14.8 %shard_map.50 = bf16[16,16,2048]{2,1,0:T(8,128)(2,1)} custom-call(bf16[16,2048]{1,0:T(8,128)(2,1)} %bitcast.13), custom_call_target="tpu_custom_call" | custom-call | tf_op jit(solution)/shard_map/pallas_call | solution.py:255
  15.5 9.8 %shard_map.51 = f32[256,2048]{1,0:T(8,128)} custom-call(s32[8,8]{1,0:T(8,128)} %mask_ref.3, bf16[2048,2048]{1,0:T(8,128)(2,1)} %g_ref.3, bf16[256,2048]{1,0:T(8,128)(2,1)} %bitcast.9), custom_call_target="tpu_custom_call" | custom-call | tf_op jit(solution)/shard_map/pallas_call | solution.py:334
  25.3 85.7 %shard_map.52 = (f32[16,2048]{1,0:T(8,128)}, bf16[16,16,2048]{2,1,0:T(8,128)(2,1)}) custom-call(f32[16,16,2048]{2,1,0:T(8,128)} %bitcast.7), custom_call_target="tpu_custom_call" | custom-call | tf_op jit(solution)/shard_map/pallas_call | solution.py:203
  110.9 9.7 %shard_map.53 = f32[256,2048]{1,0:T(8,128)} custom-call(s32[8,8]{1,0:T(8,128)} %mask_ref.3, bf16[256,2048]{1,0:T(8,128)(2,1)} %bitcast.10, bf16[2048,2048]{1,0:T(8,128)(2,1)} %g_ref.3), custom_call_target="tpu_custom_call" | custom-call | tf_op jit(solution)/shard_map/pallas_call | solution.py:353
  120.6 0.0 copy-start
  120.6 25.0 %shard_map.54 = f32[16,2048]{1,0:T(8,128)} custom-call(f32[16,16,2048]{2,1,0:T(8,128)} %bitcast.8), custom_call_target="tpu_custom_call" | custom-call | tf_op jit(solution)/shard_map/pallas_call | solution.py:235
  145.6 0.0 copy-done
  145.6 0.7 copy.7
  146.3 1.6 %copy.8 = f32[2048,16]{0,1:T(8,128)} copy(f32[2048,16]{0,1:T(8,128)} %bitcast.11) | data formatting | bytes 262144
Async XLA Ops:
  120.6 25.0 %copy-start = (f32[16,2048]{1,0:T(8,128)S(1)}, f32[16,2048]{1,0:T(8,128)}, u32[]{:S(2)}) copy-start(f32[16,2048]{1,0:T(8,128)} %get-tuple-element.4) | copy-start | bytes 393220

commit v9 on v7

--- a/solution.py
+++ b/solution.py
@@ -297,37 +297,46 @@
     return keep != 0
 
 
-def _sketch_kernel(nb, bs, mask_ref, g_ref, p_ref, o_ref):
+def _sub_blocks(nb):
+    return 4 if nb % 4 == 0 else (2 if nb % 2 == 0 else 1)
+
+
+def _sketch_kernel(nb, bs, sub, mask_ref, g_ref, p_ref, o_ref):
     i = pl.program_id(0)
-    keep = _mask_lanes(mask_ref, nb, bs, p_ref.shape[1], row=i)
-    p = jnp.where(keep, p_ref[...], jnp.zeros_like(p_ref))
-    o_ref[...] = lax.dot_general(
-        p, g_ref[...], (((1,), (1,)), ((), ())), preferred_element_type=jnp.float32
-    )
-
-
-def _adjoint_kernel(nb, bs, mask_ref, l_ref, g_ref, o_ref):
+    for h in range(sub):
+        keep = _mask_lanes(mask_ref, nb, bs, p_ref.shape[1], row=i * sub + h)
+        p = jnp.where(keep, p_ref[...], jnp.zeros_like(p_ref))
+        o_ref[:, h * bs:(h + 1) * bs] = lax.dot_general(
+            p, g_ref[h * bs:(h + 1) * bs, :], (((1,), (1,)), ((), ())), preferred_element_type=jnp.float32
+        )
+
+
+def _adjoint_kernel(nb, bs, sub, mask_ref, l_ref, g_ref, o_ref):
     j = pl.program_id(0)
-    keep = _mask_lanes(mask_ref, nb, bs, l_ref.shape[1], col=j)
-    lowered = jnp.where(keep, l_ref[...], jnp.zeros_like(l_ref))
-    o_ref[...] = jnp.dot(lowered, g_ref[...], preferred_element_type=jnp.float32)
+    for h in range(sub):
+        keep = _mask_lanes(mask_ref, nb, bs, l_ref.shape[1], col=j * sub + h)
+        lowered = jnp.where(keep, l_ref[...], jnp.zeros_like(l_ref))
+        o_ref[:, h * bs:(h + 1) * bs] = jnp.dot(
+            lowered, g_ref[:, h * bs:(h + 1) * bs], preferred_element_type=jnp.float32
+        )
 
 
 def _sketch_partial(mask, green, probes_t):
     rb, cb = mask.shape
     bs = green.shape[0] // rb
+    sub = _sub_blocks(rb)
     k = probes_t.shape[0]
     return pl.pallas_call(
-        functools.partial(_sketch_kernel, cb, bs),
+        functools.partial(_sketch_kernel, cb, bs, sub),
         out_shape=jax.ShapeDtypeStruct((k, green.shape[0]), jnp.float32),
         grid_spec=pltpu.PrefetchScalarGridSpec(
             num_scalar_prefetch=1,
-            grid=(rb,),
+            grid=(rb // sub,),
             in_specs=[
-                pl.BlockSpec((bs, green.shape[1]), lambda i, m: (i, 0)),
+                pl.BlockSpec((bs * sub, green.shape[1]), lambda i, m: (i, 0)),
                 pl.BlockSpec((k, green.shape[1]), lambda i, m: (0, 0)),
             ],
-            out_specs=pl.BlockSpec((k, bs), lambda i, m: (0, i)),
+            out_specs=pl.BlockSpec((k, bs * sub), lambda i, m: (0, i)),
         ),
     )(mask, green, probes_t)
 
@@ -335,18 +344,19 @@
 def _adjoint_partial(mask, lowered_t, green):
     rb, cb = mask.shape
     bs = green.shape[0] // rb
+    sub = _sub_blocks(cb)
     k = lowered_t.shape[0]
     return pl.pallas_call(
-        functools.partial(_adjoint_kernel, rb, bs),
+        functools.partial(_adjoint_kernel, rb, bs, sub),
         out_shape=jax.ShapeDtypeStruct((k, green.shape[1]), jnp.float32),
         grid_spec=pltpu.PrefetchScalarGridSpec(
             num_scalar_prefetch=1,
-            grid=(cb,),
+            grid=(cb // sub,),
             in_specs=[
                 pl.BlockSpec((k, green.shape[0]), lambda j, m: (0, 0)),
-                pl.BlockSpec((green.shape[0], bs), lambda j, m: (0, j)),
+                pl.BlockSpec((green.shape[0], bs * sub), lambda j, m: (0, j)),
             ],
-            out_specs=pl.BlockSpec((k, bs), lambda j, m: (0, j)),
+            out_specs=pl.BlockSpec((k, bs * sub), lambda j, m: (0, j)),
         ),
     )(mask, lowered_t, green)
 

time: 142 us -> 135 us (0.951)
  Pallas kernels: 138 us -> 132 us
    pallas_call x2, Pallas kernels: 19.5 us -> 13.5 us  [the longest x1 6.76 us: _sketch_partial(): pl.pallas_call(functools.partial(_sketch_kernel, cb, bs, sub), out_shape=...]
where the time goes in v9:
time: 135 us
  Pallas kernels  132 us (98%)
  local copies, waits for them, and re-layouts  2.23 us (2%)
    pallas_call x1, Pallas kernels, _all_reduce(): pl.pallas_call(functools.partial(_ar_kernel, axis, other_axis, chips), ou...  80.7 us
    pallas_call x1, Pallas kernels, _row_reduce_scatter(): pl.pallas_call(functools.partial(_row_rs_kernel, axis, other_axis, chips)...  23.2 us
    pallas_call x1, Pallas kernels, _row_all_gather(): pl.pallas_call(functools.partial(_row_ag_kernel, axis, other_axis, chips)...  14.8 us
    pallas_call x1, Pallas kernels, _sketch_partial(): pl.pallas_call(functools.partial(_sketch_kernel, cb, bs, sub), out_shape=...  6.76 us
    pallas_call x1, Pallas kernels, _adjoint_partial(): pl.pallas_call(functools.partial(_adjoint_kernel, rb, bs, sub), out_shape...  6.72 us

profile of v9, /device:TPU:27, one launch (start us, length us, event | category | flops | bytes accessed | tf_op | source)
XLA Modules:
  0.0 135.1 jit_solution(1035918990739417056)
XLA Ops:
  0.6 14.8 %shard_map.50 = bf16[8,2,16,2048]{3,2,1,0:T(8,128)(2,1)} custom-call(bf16[16,2048]{1,0:T(8,128)(2,1)} %bitcast.13), custom_call_target="tpu_custom_call" | custom-call | tf_op jit(solution)/shard_map/pallas_call | solution.py:241
  15.4 6.8 %shard_map.51 = f32[256,2048]{1,0:T(8,128)} custom-call(s32[8,8]{1,0:T(8,128)} %mask_ref.3, bf16[2048,2048]{1,0:T(8,128)(2,1)} %g_ref.3, bf16[256,2048]{1,0:T(8,128)(2,1)} %bitcast.9), custom_call_target="tpu_custom_call" | custom-call | tf_op jit(solution)/shard_map/pallas_call | solution.py:329
  22.2 80.7 %shard_map.52 = (f32[16,2048]{1,0:T(8,128)}, bf16[8,2,16,2048]{3,2,1,0:T(8,128)(2,1)}) custom-call(f32[8,2,16,2048]{3,2,1,0:T(8,128)} %bitcast.7), custom_call_target="tpu_custom_call" | custom-call | tf_op jit(solution)/shard_map/pallas_call | solution.py:190
  102.9 6.7 %shard_map.53 = f32[256,2048]{1,0:T(8,128)} custom-call(s32[8,8]{1,0:T(8,128)} %mask_ref.3, bf16[256,2048]{1,0:T(8,128)(2,1)} %bitcast.10, bf16[2048,2048]{1,0:T(8,128)(2,1)} %g_ref.3), custom_call_target="tpu_custom_call" | custom-call | tf_op jit(solution)/shard_map/pallas_call | solution.py:349
  109.6 0.0 copy-start
  109.6 23.2 %shard_map.54 = f32[16,2048]{1,0:T(8,128)} custom-call(f32[8,2,16,2048]{3,2,1,0:T(8,128)} %bitcast.8), custom_call_target="tpu_custom_call" | custom-call | tf_op jit(solution)/shard_map/pallas_call | solution.py:221
  132.9 0.0 copy-done
  132.9 0.7 copy.7
  133.5 1.6 %copy.8 = f32[2048,16]{0,1:T(8,128)} copy(f32[2048,16]{0,1:T(8,128)} %bitcast.11) | data formatting | bytes 262144
Async XLA Ops:
  109.6 23.3 %copy-start = (f32[16,2048]{1,0:T(8,128)S(1)}, f32[16,2048]{1,0:T(8,128)}, u32[]{:S(2)}) copy-start(f32[16,2048]{1,0:T(8,128)} %get-tuple-element.4) | copy-start | bytes 393220

commit v10 on v9

--- a/solution.py
+++ b/solution.py
@@ -71,6 +71,10 @@
         o_ref[lax.rem(me + n - 1 - d, n)] = recv[d]
     for copy in copies:
         copy.wait_send()
+
+
+def _index(axis, group, bit):
+    return group * 2 + bit
 
 
 def _row_greet(axis, me, other, chips):
@@ -175,42 +179,115 @@
         copy.wait_send()
 
 
+def _col_rs_body(axis, other, chips, chip, core, x_ref, o_ref, recv1, mid, recv2, s1, r1, s2, r2):
+    sib = _peer(axis, other, _index(axis, chip, 1 - core))
+    first = []
+    for d in range(1, chips):
+        target = lax.rem(chip + d, chips)
+        for half, bit in enumerate((core, 1 - core)):
+            copy = pltpu.make_async_remote_copy(
+                src_ref=x_ref.at[_index(axis, target, bit)],
+                dst_ref=recv1.at[d - 1, half],
+                send_sem=s1.at[d - 1, half],
+                recv_sem=r1.at[d - 1, half],
+                device_id=_peer(axis, other, _index(axis, target, core)),
+                device_id_type=MESH,
+            )
+            copy.start()
+            first.append(copy)
+    for copy in first:
+        copy.wait_recv()
+    part = x_ref[_index(axis, chip, 1 - core)]
+    for d in range(chips - 1):
+        part = part + recv1[d, 1]
+    mid[...] = part
+    last = pltpu.make_async_remote_copy(
+        src_ref=mid, dst_ref=recv2, send_sem=s2.at[0], recv_sem=r2.at[0],
+        device_id=sib, device_id_type=MESH,
+    )
+    last.start()
+    acc = x_ref[_index(axis, chip, core)]
+    for d in range(chips - 1):
+        acc = acc + recv1[d, 0]
+    last.wait_recv()
+    o_ref[...] = acc + recv2[...]
+    for copy in first + [last]:
+        copy.wait_send()
+
+
+def _col_ag_body(axis, other, chips, chip, core, x_ref, o_ref, recv_s, recv_a, s1, r1, s2, r2):
+    sib = _peer(axis, other, _index(axis, chip, 1 - core))
+    to_sib = pltpu.make_async_remote_copy(
+        src_ref=x_ref, dst_ref=recv_s, send_sem=s1.at[0], recv_sem=r1.at[0],
+        device_id=sib, device_id_type=MESH,
+    )
+    to_sib.start()
+    sends = []
+    for d in range(1, chips):
+        peer = _peer(axis, other, _index(axis, lax.rem(chip + d, chips), core))
+        copy = pltpu.make_async_remote_copy(
+            src_ref=x_ref, dst_ref=recv_a.at[d - 1, 0], send_sem=s2.at[d - 1, 0],
+            recv_sem=r2.at[d - 1, 0], device_id=peer, device_id_type=MESH,
+        )
+        copy.start()
+        sends.append(copy)
+    o_ref[_index(axis, chip, core)] = x_ref[...]
+    to_sib.wait_recv()
+    for d in range(1, chips):
+        peer = _peer(axis, other, _index(axis, lax.rem(chip + d, chips), core))
+        copy = pltpu.make_async_remote_copy(
+            src_ref=recv_s, dst_ref=recv_a.at[d - 1, 1], send_sem=s2.at[d - 1, 1],
+            recv_sem=r2.at[d - 1, 1], device_id=peer, device_id_type=MESH,
+        )
+        copy.start()
+        sends.append(copy)
+    o_ref[_index(axis, chip, 1 - core)] = recv_s[...]
+    for copy in sends:
+        copy.wait_recv()
+    for d in range(1, chips):
+        source = lax.rem(chip + chips - d, chips)
+        o_ref[_index(axis, source, core)] = recv_a[d - 1, 0]
+        o_ref[_index(axis, source, 1 - core)] = recv_a[d - 1, 1]
+    for copy in [to_sib] + sends:
+        copy.wait_send()
+
+
 def _ar_kernel(axis, other_axis, chips, x_ref, o_ref, g_ref, low, *scratch):
     me = lax.axis_index(axis)
     other = lax.axis_index(other_axis)
     chip, core = _row_greet(axis, me, other, chips)
-    _rs_body(axis, other, chips, chip, core, x_ref, o_ref, *scratch[:7])
+    _col_rs_body(axis, other, chips, chip, core, x_ref, o_ref, *scratch[:7])
     low[...] = o_ref[...].astype(low.dtype)
-    _ag_body(axis, other, chips, chip, core, low, g_ref, *scratch[7:])
+    _col_ag_body(axis, other, chips, chip, core, low, g_ref, *scratch[7:])
 
 
 def _all_reduce(x, axis, other_axis, collective_id):
-    chips, _, rows, width = x.shape
+    n, rows, width = x.shape
+    chips = n // 2
     low = jnp.bfloat16
     return pl.pallas_call(
         functools.partial(_ar_kernel, axis, other_axis, chips),
         out_shape=(
             jax.ShapeDtypeStruct((rows, width), x.dtype),
-            jax.ShapeDtypeStruct((chips, 2, rows, width), low),
+            jax.ShapeDtypeStruct((n, rows, width), low),
         ),
         in_specs=[pl.BlockSpec(memory_space=pltpu.VMEM)],
         out_specs=(pl.BlockSpec(memory_space=pltpu.VMEM), pl.BlockSpec(memory_space=pltpu.VMEM)),
         scratch_shapes=[
             pltpu.VMEM((rows, width), low),
-            pltpu.VMEM((chips, rows, width), x.dtype),
-            pltpu.VMEM((chips - 1, rows, width), x.dtype),
-            pltpu.VMEM((chips - 1, rows, width), x.dtype),
-            pltpu.SemaphoreType.DMA((chips,)),
-            pltpu.SemaphoreType.DMA((chips,)),
-            pltpu.SemaphoreType.DMA((chips - 1,)),
-            pltpu.SemaphoreType.DMA((chips - 1,)),
+            pltpu.VMEM((chips - 1, 2, rows, width), x.dtype),
+            pltpu.VMEM((rows, width), x.dtype),
+            pltpu.VMEM((rows, width), x.dtype),
+            pltpu.SemaphoreType.DMA((chips - 1, 2)),
+            pltpu.SemaphoreType.DMA((chips - 1, 2)),
+            pltpu.SemaphoreType.DMA((1,)),
+            pltpu.SemaphoreType.DMA((1,)),
             pltpu.VMEM((rows, width), low),
-            pltpu.VMEM((chips - 1, rows, width), low),
-            pltpu.VMEM((chips - 1, rows, width), low),
-            pltpu.SemaphoreType.DMA((chips,)),
-            pltpu.SemaphoreType.DMA((chips,)),
-            pltpu.SemaphoreType.DMA((chips - 1,)),
-            pltpu.SemaphoreType.DMA((chips - 1,)),
+            pltpu.VMEM((chips - 1, 2, rows, width), low),
+            pltpu.SemaphoreType.DMA((1,)),
+            pltpu.SemaphoreType.DMA((1,)),
+            pltpu.SemaphoreType.DMA((chips - 1, 2)),
+            pltpu.SemaphoreType.DMA((chips - 1, 2)),
         ],
         compiler_params=pltpu.CompilerParams(collective_id=collective_id, has_side_effects=True),
     )(x)
@@ -368,7 +445,7 @@
     k = n_row * probes_t.shape[2]
     probes_t = probes_t.reshape(k, -1)
     partial_t = _sketch_partial(mask, green, probes_t)
-    sketch_t, lowered_t = _all_reduce(partial_t.reshape(n_col // 2, 2, k // n_col, -1), "col", "row", 0)
+    sketch_t, lowered_t = _all_reduce(partial_t.reshape(n_col, k // n_col, -1), "col", "row", 0)
     lowered_t = lowered_t.reshape(k, -1)
     term_t = _adjoint_partial(mask, lowered_t, green)
     adjoint_t = _row_reduce_scatter(term_t.reshape(n_row // 2, 2, k // n_row, -1), "row", "col", 2)

time: 135 us -> 141 us (1.044)
  the two profiles are of different devices: /device:TPU:27 before, /device:TPU:93 now
where the time goes in v10:
time: 141 us; the launch traced here: 140 us
  Pallas kernels  137 us (97%)
  local copies, waits for them, and re-layouts  2.23 us (2%)
    pallas_call x1, Pallas kernels, _all_reduce(): pl.pallas_call(functools.partial(_ar_kernel, axis, other_axis, chips), ou...  84.8 us
    pallas_call x1, Pallas kernels, _row_reduce_scatter(): pl.pallas_call(functools.partial(_row_rs_kernel, axis, other_axis, chips)...  23.6 us
    pallas_call x1, Pallas kernels, _row_all_gather(): pl.pallas_call(functools.partial(_row_ag_kernel, axis, other_axis, chips)...  14.8 us
    pallas_call x1, Pallas kernels, _sketch_partial(): pl.pallas_call(functools.partial(_sketch_kernel, cb, bs, sub), out_shape=...  6.76 us
    pallas_call x1, Pallas kernels, _adjoint_partial(): pl.pallas_call(functools.partial(_adjoint_kernel, rb, bs, sub), out_shape...  6.72 us

profile of v10, /device:TPU:93, one launch (start us, length us, event | category | flops | bytes accessed | tf_op | source)
XLA Modules:
  0.0 139.6 jit_solution(15514534217102377056)
XLA Ops:
  0.6 14.8 %shard_map.50 = bf16[8,2,16,2048]{3,2,1,0:T(8,128)(2,1)} custom-call(bf16[16,2048]{1,0:T(8,128)(2,1)} %bitcast.13), custom_call_target="tpu_custom_call" | custom-call | tf_op jit(solution)/shard_map/pallas_call | solution.py:318
  15.4 6.8 %shard_map.51 = f32[256,2048]{1,0:T(8,128)} custom-call(s32[8,8]{1,0:T(8,128)} %mask_ref.3, bf16[2048,2048]{1,0:T(8,128)(2,1)} %g_ref.3, bf16[256,2048]{1,0:T(8,128)(2,1)} %bitcast.9), custom_call_target="tpu_custom_call" | custom-call | tf_op jit(solution)/shard_map/pallas_call | solution.py:406
  22.2 84.8 %shard_map.52 = (f32[16,2048]{1,0:T(8,128)}, bf16[16,16,2048]{2,1,0:T(8,128)(2,1)}) custom-call(f32[16,16,2048]{2,1,0:T(8,128)} %bitcast.7), custom_call_target="tpu_custom_call" | custom-call | tf_op jit(solution)/shard_map/pallas_call | solution.py:268
  107.0 6.7 %shard_map.53 = f32[256,2048]{1,0:T(8,128)} custom-call(s32[8,8]{1,0:T(8,128)} %mask_ref.3, bf16[256,2048]{1,0:T(8,128)(2,1)} %bitcast.10, bf16[2048,2048]{1,0:T(8,128)(2,1)} %g_ref.3), custom_call_target="tpu_custom_call" | custom-call | tf_op jit(solution)/shard_map/pallas_call | solution.py:426
  113.7 0.0 copy-start
  113.7 23.6 %shard_map.54 = f32[16,2048]{1,0:T(8,128)} custom-call(f32[8,2,16,2048]{3,2,1,0:T(8,128)} %bitcast.8), custom_call_target="tpu_custom_call" | custom-call | tf_op jit(solution)/shard_map/pallas_call | solution.py:298
  137.4 0.0 copy-done
  137.4 0.7 copy.7
  138.0 1.6 %copy.8 = f32[2048,16]{0,1:T(8,128)} copy(f32[2048,16]{0,1:T(8,128)} %bitcast.11) | data formatting | bytes 262144
Async XLA Ops:
  113.7 23.6 %copy-start = (f32[16,2048]{1,0:T(8,128)S(1)}, f32[16,2048]{1,0:T(8,128)}, u32[]{:S(2)}) copy-start(f32[16,2048]{1,0:T(8,128)} %get-tuple-element.4) | copy-start | bytes 393220

commit v11 on v9

--- a/solution.py
+++ b/solution.py
@@ -175,17 +175,80 @@
         copy.wait_send()
 
 
+def _mixed_rs_body(axis, other, chips, chip, core, x_ref, o_ref, ra1, ma, ra2, rb1, mb, rb2,
+                   sa1, qa1, sa2, qa2, sb1, qb1, sb2, qb2):
+    sib = _peer(axis, other, chip * 2 + 1 - core)
+    width = x_ref.shape[-1]
+    a1 = []
+    for q in range(chips):
+        copy = pltpu.make_async_remote_copy(
+            src_ref=x_ref.at[0, q * 2 + 1 - core], dst_ref=ra1.at[q], send_sem=sa1.at[q],
+            recv_sem=qa1.at[q], device_id=sib, device_id_type=MESH,
+        )
+        copy.start()
+        a1.append(copy)
+    b1 = []
+    for d in range(1, chips):
+        target = lax.rem(chip + d, chips)
+        for half, bit in enumerate((core, 1 - core)):
+            copy = pltpu.make_async_remote_copy(
+                src_ref=x_ref.at[1, target * 2 + bit], dst_ref=rb1.at[d - 1, half],
+                send_sem=sb1.at[d - 1, half], recv_sem=qb1.at[d - 1, half],
+                device_id=_peer(axis, other, target * 2 + core), device_id_type=MESH,
+            )
+            copy.start()
+            b1.append(copy)
+    for copy in a1:
+        copy.wait_recv()
+    a2 = []
+    for d in range(1, chips):
+        target = lax.rem(chip + d, chips)
+        ma[d - 1] = x_ref[0, target * 2 + core] + ra1[target]
+        copy = pltpu.make_async_remote_copy(
+            src_ref=ma.at[d - 1], dst_ref=ra2.at[d - 1], send_sem=sa2.at[d - 1],
+            recv_sem=qa2.at[d - 1], device_id=_peer(axis, other, target * 2 + core),
+            device_id_type=MESH,
+        )
+        copy.start()
+        a2.append(copy)
+    for copy in b1:
+        copy.wait_recv()
+    part = x_ref[1, chip * 2 + 1 - core]
+    for d in range(chips - 1):
+        part = part + rb1[d, 1]
+    mb[...] = part
+    b2 = pltpu.make_async_remote_copy(
+        src_ref=mb, dst_ref=rb2, send_sem=sb2.at[0], recv_sem=qb2.at[0],
+        device_id=sib, device_id_type=MESH,
+    )
+    b2.start()
+    acc_b = x_ref[1, chip * 2 + core]
+    for d in range(chips - 1):
+        acc_b = acc_b + rb1[d, 0]
+    acc_a = x_ref[0, chip * 2 + core] + ra1[chip]
+    for d, copy in enumerate(a2):
+        copy.wait_recv()
+        acc_a = acc_a + ra2[d]
+    b2.wait_recv()
+    o_ref[:, :width] = acc_a
+    o_ref[:, width:] = acc_b + rb2[...]
+    for copy in a1 + b1 + a2 + [b2]:
+        copy.wait_send()
+
+
 def _ar_kernel(axis, other_axis, chips, x_ref, o_ref, g_ref, low, *scratch):
     me = lax.axis_index(axis)
     other = lax.axis_index(other_axis)
     chip, core = _row_greet(axis, me, other, chips)
-    _rs_body(axis, other, chips, chip, core, x_ref, o_ref, *scratch[:7])
+    _mixed_rs_body(axis, other, chips, chip, core, x_ref, o_ref, *scratch[:14])
     low[...] = o_ref[...].astype(low.dtype)
-    _ag_body(axis, other, chips, chip, core, low, g_ref, *scratch[7:])
+    _ag_body(axis, other, chips, chip, core, low, g_ref, *scratch[14:])
 
 
 def _all_reduce(x, axis, other_axis, collective_id):
-    chips, _, rows, width = x.shape
+    _, n, rows, half = x.shape
+    chips = n // 2
+    width = 2 * half
     low = jnp.bfloat16
     return pl.pallas_call(
         functools.partial(_ar_kernel, axis, other_axis, chips),
@@ -197,13 +260,20 @@
         out_specs=(pl.BlockSpec(memory_space=pltpu.VMEM), pl.BlockSpec(memory_space=pltpu.VMEM)),
         scratch_shapes=[
             pltpu.VMEM((rows, width), low),
-            pltpu.VMEM((chips, rows, width), x.dtype),
-            pltpu.VMEM((chips - 1, rows, width), x.dtype),
-            pltpu.VMEM((chips - 1, rows, width), x.dtype),
-            pltpu.SemaphoreType.DMA((chips,)),
-            pltpu.SemaphoreType.DMA((chips,)),
-            pltpu.SemaphoreType.DMA((chips - 1,)),
-            pltpu.SemaphoreType.DMA((chips - 1,)),
+            pltpu.VMEM((chips, rows, half), x.dtype),
+            pltpu.VMEM((chips - 1, rows, half), x.dtype),
+            pltpu.VMEM((chips - 1, rows, half), x.dtype),
+            pltpu.VMEM((chips - 1, 2, rows, half), x.dtype),
+            pltpu.VMEM((rows, half), x.dtype),
+            pltpu.VMEM((rows, half), x.dtype),
+            pltpu.SemaphoreType.DMA((chips,)),
+            pltpu.SemaphoreType.DMA((chips,)),
+            pltpu.SemaphoreType.DMA((chips - 1,)),
+            pltpu.SemaphoreType.DMA((chips - 1,)),
+            pltpu.SemaphoreType.DMA((chips - 1, 2)),
+            pltpu.SemaphoreType.DMA((chips - 1, 2)),
+            pltpu.SemaphoreType.DMA((1,)),
+            pltpu.SemaphoreType.DMA((1,)),
             pltpu.VMEM((rows, width), low),
             pltpu.VMEM((chips - 1, rows, width), low),
             pltpu.VMEM((chips - 1, rows, width), low),
@@ -301,6 +371,10 @@
     return 4 if nb % 4 == 0 else (2 if nb % 2 == 0 else 1)
 
 
+def _half_blocks(nb):
+    return nb // 2
+
+
 def _sketch_kernel(nb, bs, sub, mask_ref, g_ref, p_ref, o_ref):
     i = pl.program_id(0)
     for h in range(sub):
@@ -324,11 +398,11 @@
 def _sketch_partial(mask, green, probes_t):
     rb, cb = mask.shape
     bs = green.shape[0] // rb
-    sub = _sub_blocks(rb)
+    sub = _half_blocks(rb)
     k = probes_t.shape[0]
     return pl.pallas_call(
         functools.partial(_sketch_kernel, cb, bs, sub),
-        out_shape=jax.ShapeDtypeStruct((k, green.shape[0]), jnp.float32),
+        out_shape=jax.ShapeDtypeStruct((rb // sub, k, bs * sub), jnp.float32),
         grid_spec=pltpu.PrefetchScalarGridSpec(
             num_scalar_prefetch=1,
             grid=(rb // sub,),
@@ -336,7 +410,7 @@
                 pl.BlockSpec((bs * sub, green.shape[1]), lambda i, m: (i, 0)),
                 pl.BlockSpec((k, green.shape[1]), lambda i, m: (0, 0)),
             ],
-            out_specs=pl.BlockSpec((k, bs * sub), lambda i, m: (0, i)),
+            out_specs=pl.BlockSpec((None, k, bs * sub), lambda i, m: (i, 0, 0)),
         ),
     )(mask, green, probes_t)
 
@@ -368,7 +442,7 @@
     k = n_row * probes_t.shape[2]
     probes_t = probes_t.reshape(k, -1)
     partial_t = _sketch_partial(mask, green, probes_t)
-    sketch_t, lowered_t = _all_reduce(partial_t.reshape(n_col // 2, 2, k // n_col, -1), "col", "row", 0)
+    sketch_t, lowered_t = _all_reduce(partial_t.reshape(2, n_col, k // n_col, -1), "col", "row", 0)
     lowered_t = lowered_t.reshape(k, -1)
     term_t = _adjoint_partial(mask, lowered_t, green)
     adjoint_t = _row_reduce_scatter(term_t.reshape(n_row // 2, 2, k // n_row, -1), "row", "col", 2)

time: 135 us -> 121 us (0.90)
  the two profiles are of different devices: /device:TPU:27 before, /device:TPU:93 now
where the time goes in v11:
time: 121 us; the launch traced here: 119 us
  Pallas kernels  116 us (96%)
  local copies, waits for them, and re-layouts  2.23 us (2%)
    pallas_call x1, Pallas kernels, _all_reduce(): pl.pallas_call(functools.partial(_ar_kernel, axis, other_axis, chips), ou...  64.6 us
    pallas_call x1, Pallas kernels, _row_reduce_scatter(): pl.pallas_call(functools.partial(_row_rs_kernel, axis, other_axis, chips)...  23.1 us
    pallas_call x1, Pallas kernels, _row_all_gather(): pl.pallas_call(functools.partial(_row_ag_kernel, axis, other_axis, chips)...  14.8 us
    pallas_call x1, Pallas kernels, _sketch_partial(): pl.pallas_call(functools.partial(_sketch_kernel, cb, bs, sub), out_shape=...  6.83 us
    pallas_call x1, Pallas kernels, _adjoint_partial(): pl.pallas_call(functools.partial(_adjoint_kernel, rb, bs, sub), out_shape...  6.72 us

profile of v11, /device:TPU:93, one launch (start us, length us, event | category | flops | bytes accessed | tf_op | source)
XLA Modules:
  0.0 118.9 jit_solution(2098719349423229167)
XLA Ops:
  0.6 14.8 %shard_map.50 = bf16[8,2,16,2048]{3,2,1,0:T(8,128)(2,1)} custom-call(bf16[16,2048]{1,0:T(8,128)(2,1)} %bitcast.13), custom_call_target="tpu_custom_call" | custom-call | tf_op jit(solution)/shard_map/pallas_call | solution.py:311
  15.4 6.8 %shard_map.51 = f32[2,256,1024]{2,1,0:T(8,128)} custom-call(s32[8,8]{1,0:T(8,128)} %mask_ref.3, bf16[2048,2048]{1,0:T(8,128)(2,1)} %g_ref.3, bf16[256,2048]{1,0:T(8,128)(2,1)} %bitcast.9), custom_call_target="tpu_custom_call" | custom-call | tf_op jit(solution)/shard_map/pallas_call | solution.py:403
  22.3 64.6 %shard_map.52 = (f32[16,2048]{1,0:T(8,128)}, bf16[8,2,16,2048]{3,2,1,0:T(8,128)(2,1)}) custom-call(f32[2,16,16,1024]{3,2,1,0:T(8,128)} %bitcast.7), custom_call_target="tpu_custom_call" | custom-call | tf_op jit(solution)/shard_map/pallas_call | solution.py:253
  86.9 6.7 %shard_map.53 = f32[256,2048]{1,0:T(8,128)} custom-call(s32[8,8]{1,0:T(8,128)} %mask_ref.3, bf16[256,2048]{1,0:T(8,128)(2,1)} %bitcast.10, bf16[2048,2048]{1,0:T(8,128)(2,1)} %g_ref.3), custom_call_target="tpu_custom_call" | custom-call | tf_op jit(solution)/shard_map/pallas_call | solution.py:423
  93.6 0.0 copy-start
  93.6 23.1 %shard_map.54 = f32[16,2048]{1,0:T(8,128)} custom-call(f32[8,2,16,2048]{3,2,1,0:T(8,128)} %bitcast.8), custom_call_target="tpu_custom_call" | custom-call | tf_op jit(solution)/shard_map/pallas_call | solution.py:291
  116.7 0.0 copy-done
  116.7 0.7 copy.7
  117.4 1.6 %copy.8 = f32[2048,16]{0,1:T(8,128)} copy(f32[2048,16]{0,1:T(8,128)} %bitcast.11) | data formatting | bytes 262144
Async XLA Ops:
  93.6 23.1 %copy-start = (f32[16,2048]{1,0:T(8,128)S(1)}, f32[16,2048]{1,0:T(8,128)}, u32[]{:S(2)}) copy-start(f32[16,2048]{1,0:T(8,128)} %get-tuple-element.4) | copy-start | bytes 393220

commit v12 on v11

--- a/solution.py
+++ b/solution.py
@@ -236,13 +236,79 @@
         copy.wait_send()
 
 
+def _mixed_ag_body(axis, other, chips, chip, core, low, o_ref, ra, fa, rbs, rb,
+                   sa, qa, sf, qf, ss, qs, sb, qb):
+    sib = _peer(axis, other, chip * 2 + 1 - core)
+    width = low.shape[-1]
+
+    def peer(d):
+        return _peer(axis, other, lax.rem(chip + d, chips) * 2 + core)
+
+    a1 = []
+    for d in range(1, chips):
+        copy = pltpu.make_async_remote_copy(
+            src_ref=low.at[0], dst_ref=ra.at[d - 1], send_sem=sa.at[d - 1], recv_sem=qa.at[d - 1],
+            device_id=peer(d), device_id_type=MESH,
+        )
+        copy.start()
+        a1.append(copy)
+    b1 = pltpu.make_async_remote_copy(
+        src_ref=low.at[1], dst_ref=rbs, send_sem=ss.at[0], recv_sem=qs.at[0],
+        device_id=sib, device_id_type=MESH,
+    )
+    b1.start()
+    own_a = pltpu.make_async_remote_copy(
+        src_ref=low.at[0], dst_ref=fa.at[chips - 1], send_sem=sf.at[chips - 1],
+        recv_sem=qf.at[chips - 1], device_id=sib, device_id_type=MESH,
+    )
+    own_a.start()
+    me = chip * 2 + core
+    o_ref[me, :, :width] = low[0]
+    o_ref[me, :, width:] = low[1]
+    b1.wait_recv()
+    b2 = []
+    for d in range(1, chips):
+        for half, src in enumerate((low.at[1], rbs)):
+            copy = pltpu.make_async_remote_copy(
+                src_ref=src, dst_ref=rb.at[d - 1, half], send_sem=sb.at[d - 1, half],
+                recv_sem=qb.at[d - 1, half], device_id=peer(d), device_id_type=MESH,
+            )
+            copy.start()
+            b2.append(copy)
+    a2 = []
+    for d in range(1, chips):
+        a1[d - 1].wait_recv()
+        copy = pltpu.make_async_remote_copy(
+            src_ref=ra.at[d - 1], dst_ref=fa.at[d - 1], send_sem=sf.at[d - 1], recv_sem=qf.at[d - 1],
+            device_id=sib, device_id_type=MESH,
+        )
+        copy.start()
+        a2.append(copy)
+    mate = chip * 2 + 1 - core
+    o_ref[mate, :, width:] = rbs[...]
+    own_a.wait_recv()
+    o_ref[mate, :, :width] = fa[chips - 1]
+    for copy in a2 + b2:
+        copy.wait_recv()
+    for d in range(1, chips):
+        source = lax.rem(chip + chips - d, chips)
+        o_ref[source * 2 + core, :, :width] = ra[d - 1]
+        o_ref[source * 2 + core, :, width:] = rb[d - 1, 0]
+        o_ref[source * 2 + 1 - core, :, :width] = fa[d - 1]
+        o_ref[source * 2 + 1 - core, :, width:] = rb[d - 1, 1]
+    for copy in a1 + [b1, own_a] + b2 + a2:
+        copy.wait_send()
+
+
 def _ar_kernel(axis, other_axis, chips, x_ref, o_ref, g_ref, low, *scratch):
     me = lax.axis_index(axis)
     other = lax.axis_index(other_axis)
     chip, core = _row_greet(axis, me, other, chips)
     _mixed_rs_body(axis, other, chips, chip, core, x_ref, o_ref, *scratch[:14])
-    low[...] = o_ref[...].astype(low.dtype)
-    _ag_body(axis, other, chips, chip, core, low, g_ref, *scratch[14:])
+    half = low.shape[-1]
+    low[0] = o_ref[:, :half].astype(low.dtype)
+    low[1] = o_ref[:, half:].astype(low.dtype)
+    _mixed_ag_body(axis, other, chips, chip, core, low, g_ref, *scratch[14:])
 
 
 def _all_reduce(x, axis, other_axis, collective_id):
@@ -254,12 +320,12 @@
         functools.partial(_ar_kernel, axis, other_axis, chips),
         out_shape=(
             jax.ShapeDtypeStruct((rows, width), x.dtype),
-            jax.ShapeDtypeStruct((chips, 2, rows, width), low),
+            jax.ShapeDtypeStruct((n, rows, width), low),
         ),
         in_specs=[pl.BlockSpec(memory_space=pltpu.VMEM)],
         out_specs=(pl.BlockSpec(memory_space=pltpu.VMEM), pl.BlockSpec(memory_space=pltpu.VMEM)),
         scratch_shapes=[
-            pltpu.VMEM((rows, width), low),
+            pltpu.VMEM((2, rows, half), low),
             pltpu.VMEM((chips, rows, half), x.dtype),
             pltpu.VMEM((chips - 1, rows, half), x.dtype),
             pltpu.VMEM((chips - 1, rows, half), x.dtype),
@@ -274,13 +340,18 @@
             pltpu.SemaphoreType.DMA((chips - 1, 2)),
             pltpu.SemaphoreType.DMA((1,)),
             pltpu.SemaphoreType.DMA((1,)),
-            pltpu.VMEM((rows, width), low),
-            pltpu.VMEM((chips - 1, rows, width), low),
-            pltpu.VMEM((chips - 1, rows, width), low),
-            pltpu.SemaphoreType.DMA((chips,)),
-            pltpu.SemaphoreType.DMA((chips,)),
-            pltpu.SemaphoreType.DMA((chips - 1,)),
-            pltpu.SemaphoreType.DMA((chips - 1,)),
+            pltpu.VMEM((chips - 1, rows, half), low),
+            pltpu.VMEM((chips, rows, half), low),
+            pltpu.VMEM((rows, half), low),
+            pltpu.VMEM((chips - 1, 2, rows, half), low),
+            pltpu.SemaphoreType.DMA((chips - 1,)),
+            pltpu.SemaphoreType.DMA((chips - 1,)),
+            pltpu.SemaphoreType.DMA((chips,)),
+            pltpu.SemaphoreType.DMA((chips,)),
+            pltpu.SemaphoreType.DMA((1,)),
+            pltpu.SemaphoreType.DMA((1,)),
+            pltpu.SemaphoreType.DMA((chips - 1, 2)),
+            pltpu.SemaphoreType.DMA((chips - 1, 2)),
         ],
         compiler_params=pltpu.CompilerParams(collective_id=collective_id, has_side_effects=True),
     )(x)

time: 121 us -> 121 us (level); the launches traced: 119 us -> 121 us
  Pallas kernels: 116 us -> 118 us
    pallas_call x1, Pallas kernels: 23.1 us -> 24.4 us  [_row_reduce_scatter(): pl.pallas_call(functools.partial(_row_rs_kernel, axis, other_axis, chips)...]
where the time goes in v12:
time: 121 us
  Pallas kernels  118 us (98%)
  local copies, waits for them, and re-layouts  2.23 us (2%)
    pallas_call x1, Pallas kernels, _all_reduce(): pl.pallas_call(functools.partial(_ar_kernel, axis, other_axis, chips), ou...  65.4 us
    pallas_call x1, Pallas kernels, _row_reduce_scatter(): pl.pallas_call(functools.partial(_row_rs_kernel, axis, other_axis, chips)...  24.4 us
    pallas_call x1, Pallas kernels, _row_all_gather(): pl.pallas_call(functools.partial(_row_ag_kernel, axis, other_axis, chips)...  14.8 us
    pallas_call x1, Pallas kernels, _sketch_partial(): pl.pallas_call(functools.partial(_sketch_kernel, cb, bs, sub), out_shape=...  6.83 us
    pallas_call x1, Pallas kernels, _adjoint_partial(): pl.pallas_call(functools.partial(_adjoint_kernel, rb, bs, sub), out_shape...  6.72 us

profile of v12, /device:TPU:93, one launch (start us, length us, event | category | flops | bytes accessed | tf_op | source)
XLA Modules:
  0.0 121.1 jit_solution(5428570824294738080)
XLA Ops:
  0.6 14.8 %shard_map.50 = bf16[8,2,16,2048]{3,2,1,0:T(8,128)(2,1)} custom-call(bf16[16,2048]{1,0:T(8,128)(2,1)} %bitcast.13), custom_call_target="tpu_custom_call" | custom-call | tf_op jit(solution)/shard_map/pallas_call | solution.py:382
  15.4 6.8 %shard_map.51 = f32[2,256,1024]{2,1,0:T(8,128)} custom-call(s32[8,8]{1,0:T(8,128)} %mask_ref.3, bf16[2048,2048]{1,0:T(8,128)(2,1)} %g_ref.3, bf16[256,2048]{1,0:T(8,128)(2,1)} %bitcast.9), custom_call_target="tpu_custom_call" | custom-call | tf_op jit(solution)/shard_map/pallas_call | solution.py:474
  22.3 65.4 %shard_map.52 = (f32[16,2048]{1,0:T(8,128)}, bf16[16,16,2048]{2,1,0:T(8,128)(2,1)}) custom-call(f32[2,16,16,1024]{3,2,1,0:T(8,128)} %bitcast.7), custom_call_target="tpu_custom_call" | custom-call | tf_op jit(solution)/shard_map/pallas_call | solution.py:319
  87.7 6.7 %shard_map.53 = f32[256,2048]{1,0:T(8,128)} custom-call(s32[8,8]{1,0:T(8,128)} %mask_ref.3, bf16[256,2048]{1,0:T(8,128)(2,1)} %bitcast.10, bf16[2048,2048]{1,0:T(8,128)(2,1)} %g_ref.3), custom_call_target="tpu_custom_call" | custom-call | tf_op jit(solution)/shard_map/pallas_call | solution.py:494
  94.4 0.0 copy-start
  94.5 24.4 %shard_map.54 = f32[16,2048]{1,0:T(8,128)} custom-call(f32[8,2,16,2048]{3,2,1,0:T(8,128)} %bitcast.8), custom_call_target="tpu_custom_call" | custom-call | tf_op jit(solution)/shard_map/pallas_call | solution.py:362
  118.9 0.0 copy-done
  118.9 0.7 copy.7
  119.6 1.6 %copy.8 = f32[2048,16]{0,1:T(8,128)} copy(f32[2048,16]{0,1:T(8,128)} %bitcast.11) | data formatting | bytes 262144
Async XLA Ops:
  94.4 24.5 %copy-start = (f32[16,2048]{1,0:T(8,128)S(1)}, f32[16,2048]{1,0:T(8,128)}, u32[]{:S(2)}) copy-start(f32[16,2048]{1,0:T(8,128)} %get-tuple-element.4) | copy-start | bytes 393220

commit v13 on v11

--- a/solution.py
+++ b/solution.py
@@ -94,25 +94,23 @@
 def _rs_body(axis, other, chips, chip, core, x_ref, o_ref, recv1, mid, recv2, s1, r1, s2, r2):
     sib = _peer(axis, other, chip * 2 + 1 - core)
     first = []
-    for q in range(chips):
-        copy = pltpu.make_async_remote_copy(
-            src_ref=x_ref.at[q, 1 - core],
-            dst_ref=recv1.at[q],
-            send_sem=s1.at[q],
-            recv_sem=r1.at[q],
+    for d in list(range(1, chips)) + [0]:
+        target = lax.rem(chip + d, chips)
+        copy = pltpu.make_async_remote_copy(
+            src_ref=x_ref.at[target, 1 - core],
+            dst_ref=recv1.at[d],
+            send_sem=s1.at[d],
+            recv_sem=r1.at[d],
             device_id=sib,
             device_id_type=MESH,
         )
         copy.start()
         first.append(copy)
-    for q in range(chips):
-        first[q].wait_recv()
+    sends = []
     for d in range(1, chips):
         target = lax.rem(chip + d, chips)
-        mid[d - 1] = x_ref[target, core] + recv1[target]
-    sends = []
-    for d in range(1, chips):
-        target = lax.rem(chip + d, chips)
+        first[d - 1].wait_recv()
+        mid[d - 1] = x_ref[target, core] + recv1[d]
         copy = pltpu.make_async_remote_copy(
             src_ref=mid.at[d - 1],
             dst_ref=recv2.at[d - 1],
@@ -123,7 +121,8 @@
         )
         copy.start()
         sends.append(copy)
-    acc = x_ref[chip, core] + recv1[chip]
+    first[chips - 1].wait_recv()
+    acc = x_ref[chip, core] + recv1[0]
     for d, copy in enumerate(sends):
         copy.wait_recv()
         acc = acc + recv2[d]
@@ -180,10 +179,11 @@
     sib = _peer(axis, other, chip * 2 + 1 - core)
     width = x_ref.shape[-1]
     a1 = []
-    for q in range(chips):
-        copy = pltpu.make_async_remote_copy(
-            src_ref=x_ref.at[0, q * 2 + 1 - core], dst_ref=ra1.at[q], send_sem=sa1.at[q],
-            recv_sem=qa1.at[q], device_id=sib, device_id_type=MESH,
+    for d in list(range(1, chips)) + [0]:
+        target = lax.rem(chip + d, chips)
+        copy = pltpu.make_async_remote_copy(
+            src_ref=x_ref.at[0, target * 2 + 1 - core], dst_ref=ra1.at[d], send_sem=sa1.at[d],
+            recv_sem=qa1.at[d], device_id=sib, device_id_type=MESH,
         )
         copy.start()
         a1.append(copy)
@@ -198,12 +198,11 @@
             )
             copy.start()
             b1.append(copy)
-    for copy in a1:
-        copy.wait_recv()
     a2 = []
     for d in range(1, chips):
         target = lax.rem(chip + d, chips)
-        ma[d - 1] = x_ref[0, target * 2 + core] + ra1[target]
+        a1[d - 1].wait_recv()
+        ma[d - 1] = x_ref[0, target * 2 + core] + ra1[d]
         copy = pltpu.make_async_remote_copy(
             src_ref=ma.at[d - 1], dst_ref=ra2.at[d - 1], send_sem=sa2.at[d - 1],
             recv_sem=qa2.at[d - 1], device_id=_peer(axis, other, target * 2 + core),
@@ -225,7 +224,8 @@
     acc_b = x_ref[1, chip * 2 + core]
     for d in range(chips - 1):
         acc_b = acc_b + rb1[d, 0]
-    acc_a = x_ref[0, chip * 2 + core] + ra1[chip]
+    a1[chips - 1].wait_recv()
+    acc_a = x_ref[0, chip * 2 + core] + ra1[0]
     for d, copy in enumerate(a2):
         copy.wait_recv()
         acc_a = acc_a + ra2[d]

time: 121 us -> 121 us (level)
  no operation moved by 1% of the time
where the time goes in v13:
time: 121 us; the launch traced here: 119 us
  Pallas kernels  117 us (97%)
  local copies, waits for them, and re-layouts  2.23 us (2%)
    pallas_call x1, Pallas kernels, _all_reduce(): pl.pallas_call(functools.partial(_ar_kernel, axis, other_axis, chips), ou...  64.6 us
    pallas_call x1, Pallas kernels, _row_reduce_scatter(): pl.pallas_call(functools.partial(_row_rs_kernel, axis, other_axis, chips)...  23.6 us
    pallas_call x1, Pallas kernels, _row_all_gather(): pl.pallas_call(functools.partial(_row_ag_kernel, axis, other_axis, chips)...  14.8 us
    pallas_call x1, Pallas kernels, _sketch_partial(): pl.pallas_call(functools.partial(_sketch_kernel, cb, bs, sub), out_shape=...  6.83 us
    pallas_call x1, Pallas kernels, _adjoint_partial(): pl.pallas_call(functools.partial(_adjoint_kernel, rb, bs, sub), out_shape...  6.72 us

profile of v13, /device:TPU:93, one launch (start us, length us, event | category | flops | bytes accessed | tf_op | source)
XLA Modules:
  0.0 119.5 jit_solution(13119813418179843344)
XLA Ops:
  0.6 14.8 %shard_map.50 = bf16[8,2,16,2048]{3,2,1,0:T(8,128)(2,1)} custom-call(bf16[16,2048]{1,0:T(8,128)(2,1)} %bitcast.13), custom_call_target="tpu_custom_call" | custom-call | tf_op jit(solution)/shard_map/pallas_call | solution.py:311
  15.4 6.8 %shard_map.51 = f32[2,256,1024]{2,1,0:T(8,128)} custom-call(s32[8,8]{1,0:T(8,128)} %mask_ref.3, bf16[2048,2048]{1,0:T(8,128)(2,1)} %g_ref.3, bf16[256,2048]{1,0:T(8,128)(2,1)} %bitcast.9), custom_call_target="tpu_custom_call" | custom-call | tf_op jit(solution)/shard_map/pallas_call | solution.py:403
  22.3 64.6 %shard_map.52 = (f32[16,2048]{1,0:T(8,128)}, bf16[8,2,16,2048]{3,2,1,0:T(8,128)(2,1)}) custom-call(f32[2,16,16,1024]{3,2,1,0:T(8,128)} %bitcast.7), custom_call_target="tpu_custom_call" | custom-call | tf_op jit(solution)/shard_map/pallas_call | solution.py:253
  86.9 6.7 %shard_map.53 = f32[256,2048]{1,0:T(8,128)} custom-call(s32[8,8]{1,0:T(8,128)} %mask_ref.3, bf16[256,2048]{1,0:T(8,128)(2,1)} %bitcast.10, bf16[2048,2048]{1,0:T(8,128)(2,1)} %g_ref.3), custom_call_target="tpu_custom_call" | custom-call | tf_op jit(solution)/shard_map/pallas_call | solution.py:423
  93.6 0.0 copy-start
  93.6 23.6 %shard_map.54 = f32[16,2048]{1,0:T(8,128)} custom-call(f32[8,2,16,2048]{3,2,1,0:T(8,128)} %bitcast.8), custom_call_target="tpu_custom_call" | custom-call | tf_op jit(solution)/shard_map/pallas_call | solution.py:291
  117.2 0.0 copy-done
  117.3 0.7 copy.7
  117.9 1.6 %copy.8 = f32[2048,16]{0,1:T(8,128)} copy(f32[2048,16]{0,1:T(8,128)} %bitcast.11) | data formatting | bytes 262144
Async XLA Ops:
  93.6 23.6 %copy-start = (f32[16,2048]{1,0:T(8,128)S(1)}, f32[16,2048]{1,0:T(8,128)}, u32[]{:S(2)}) copy-start(f32[16,2048]{1,0:T(8,128)} %get-tuple-element.4) | copy-start | bytes 393220

commit v14 on v13

--- a/solution.py
+++ b/solution.py
@@ -236,29 +236,50 @@
         copy.wait_send()
 
 
-def _ar_kernel(axis, other_axis, chips, x_ref, o_ref, g_ref, low, *scratch):
+def _ar_kernel(axis, other_axis, chips, rb, cb, bs, mask_ref, x_ref, g_hbm, o_ref, t_ref,
+               g_vmem, g_sem, l_all, low, *scratch):
+    load = pltpu.make_async_copy(g_hbm, g_vmem, g_sem.at[0])
+    load.start()
     me = lax.axis_index(axis)
     other = lax.axis_index(other_axis)
     chip, core = _row_greet(axis, me, other, chips)
     _mixed_rs_body(axis, other, chips, chip, core, x_ref, o_ref, *scratch[:14])
     low[...] = o_ref[...].astype(low.dtype)
-    _ag_body(axis, other, chips, chip, core, low, g_ref, *scratch[14:])
-
-
-def _all_reduce(x, axis, other_axis, collective_id):
+    _ag_body(axis, other, chips, chip, core, low, l_all, *scratch[14:])
+    k = l_all.shape[0] * l_all.shape[1] * l_all.shape[2]
+    lowered = l_all[...].reshape(k, l_all.shape[3])
+    load.wait()
+    for j in range(cb):
+        keep = _mask_lanes(mask_ref, rb, bs, lowered.shape[1], col=j)
+        masked = jnp.where(keep, lowered, jnp.zeros_like(lowered))
+        t_ref[:, j * bs:(j + 1) * bs] = jnp.dot(
+            masked, g_vmem[:, j * bs:(j + 1) * bs], preferred_element_type=jnp.float32
+        )
+
+
+def _all_reduce_adjoint(x, mask, green, axis, other_axis, collective_id):
     _, n, rows, half = x.shape
     chips = n // 2
     width = 2 * half
     low = jnp.bfloat16
-    return pl.pallas_call(
-        functools.partial(_ar_kernel, axis, other_axis, chips),
+    rb, cb = mask.shape
+    bs = green.shape[0] // rb
+    return pl.pallas_call(
+        functools.partial(_ar_kernel, axis, other_axis, chips, rb, cb, bs),
         out_shape=(
             jax.ShapeDtypeStruct((rows, width), x.dtype),
-            jax.ShapeDtypeStruct((chips, 2, rows, width), low),
+            jax.ShapeDtypeStruct((n * rows, green.shape[1]), jnp.float32),
         ),
-        in_specs=[pl.BlockSpec(memory_space=pltpu.VMEM)],
+        in_specs=[
+            pl.BlockSpec(memory_space=pltpu.SMEM),
+            pl.BlockSpec(memory_space=pltpu.VMEM),
+            pl.BlockSpec(memory_space=pl.ANY),
+        ],
         out_specs=(pl.BlockSpec(memory_space=pltpu.VMEM), pl.BlockSpec(memory_space=pltpu.VMEM)),
         scratch_shapes=[
+            pltpu.VMEM(green.shape, green.dtype),
+            pltpu.SemaphoreType.DMA((1,)),
+            pltpu.VMEM((chips, 2, rows, width), low),
             pltpu.VMEM((rows, width), low),
             pltpu.VMEM((chips, rows, half), x.dtype),
             pltpu.VMEM((chips - 1, rows, half), x.dtype),
@@ -283,7 +304,7 @@
             pltpu.SemaphoreType.DMA((chips - 1,)),
         ],
         compiler_params=pltpu.CompilerParams(collective_id=collective_id, has_side_effects=True),
-    )(x)
+    )(mask, x, green)
 
 
 def _row_reduce_scatter(x, axis, other_axis, collective_id):
@@ -435,16 +456,63 @@
     )(mask, lowered_t, green)
 
 
+def _ag_sketch_kernel(chips, rb, nb, bs, sub, mask_ref, x_ref, g_hbm, o_ref, g_vmem, g_sem, p_all, *scratch):
+    load = pltpu.make_async_copy(g_hbm, g_vmem, g_sem.at[0])
+    load.start()
+    me = lax.axis_index("row")
+    other = lax.axis_index("col")
+    chip, core = _row_greet("row", me, other, chips)
+    _ag_body("row", other, chips, chip, core, x_ref, p_all, *scratch)
+    k = p_all.shape[0] * p_all.shape[1] * p_all.shape[2]
+    probes_t = p_all[...].reshape(k, p_all.shape[3])
+    load.wait()
+    for h in range(rb):
+        keep = _mask_lanes(mask_ref, nb, bs, probes_t.shape[1], row=h)
+        p = jnp.where(keep, probes_t, jnp.zeros_like(probes_t))
+        o_ref[h // sub, :, (h % sub) * bs:(h % sub + 1) * bs] = lax.dot_general(
+            p, g_vmem[h * bs:(h + 1) * bs, :], (((1,), (1,)), ((), ())), preferred_element_type=jnp.float32
+        )
+
+
+def _ag_sketch(x, mask, green, chips, collective_id):
+    rows, width = x.shape
+    rb, cb = mask.shape
+    bs = green.shape[0] // rb
+    sub = _half_blocks(rb)
+    k = 2 * chips * rows
+    return pl.pallas_call(
+        functools.partial(_ag_sketch_kernel, chips, rb, cb, bs, sub),
+        out_shape=jax.ShapeDtypeStruct((rb // sub, k, bs * sub), jnp.float32),
+        in_specs=[
+            pl.BlockSpec(memory_space=pltpu.SMEM),
+            pl.BlockSpec(memory_space=pltpu.VMEM),
+            pl.BlockSpec(memory_space=pl.ANY),
+        ],
+        out_specs=pl.BlockSpec(memory_space=pltpu.VMEM),
+        scratch_shapes=[
+            pltpu.VMEM(green.shape, green.dtype),
+            pltpu.SemaphoreType.DMA((1,)),
+            pltpu.VMEM((chips, 2, rows, width), x.dtype),
+            pltpu.VMEM((rows, width), x.dtype),
+            pltpu.VMEM((chips - 1, rows, width), x.dtype),
+            pltpu.VMEM((chips - 1, rows, width), x.dtype),
+            pltpu.SemaphoreType.DMA((chips,)),
+            pltpu.SemaphoreType.DMA((chips,)),
+            pltpu.SemaphoreType.DMA((chips - 1,)),
+            pltpu.SemaphoreType.DMA((chips - 1,)),
+        ],
+        compiler_params=pltpu.CompilerParams(collective_id=collective_id, has_side_effects=True),
+    )(mask, x, green)
+
+
 def local(green, mask, probes):
     n_row = lax.axis_size("row")
     n_col = lax.axis_size("col")
-    probes_t = _row_all_gather(probes.T, "row", "col", n_row // 2, 3)
-    k = n_row * probes_t.shape[2]
-    probes_t = probes_t.reshape(k, -1)
-    partial_t = _sketch_partial(mask, green, probes_t)
-    sketch_t, lowered_t = _all_reduce(partial_t.reshape(2, n_col, k // n_col, -1), "col", "row", 0)
-    lowered_t = lowered_t.reshape(k, -1)
-    term_t = _adjoint_partial(mask, lowered_t, green)
+    partial_t = _ag_sketch(probes.T, mask, green, n_row // 2, 3)
+    k = partial_t.shape[1]
+    sketch_t, term_t = _all_reduce_adjoint(
+        partial_t.reshape(2, n_col, k // n_col, -1), mask, green, "col", "row", 0
+    )
     adjoint_t = _row_reduce_scatter(term_t.reshape(n_row // 2, 2, k // n_row, -1), "row", "col", 2)
     return (sketch_t.T, adjoint_t.T)
 

time: 121 us -> 113 us (0.934)
  Pallas kernels: 117 us -> 109 us
    pallas_call x4 -> x2, Pallas kernels: 93 us -> 85.2 us  [the longest x1 67.6 us: _all_reduce_adjoint(): pl.pallas_call(functools.partial(_ar_kernel, axis, other_axis, chips, rb,...]
where the time goes in v14:
time: 113 us; the launch traced here: 112 us
  Pallas kernels  109 us (96%)
  local copies, waits for them, and re-layouts  2.23 us (2%)
    pallas_call x1, Pallas kernels, _all_reduce_adjoint(): pl.pallas_call(functools.partial(_ar_kernel, axis, other_axis, chips, rb,...  67.6 us
    pallas_call x1, Pallas kernels, _row_reduce_scatter(): pl.pallas_call(functools.partial(_row_rs_kernel, axis, other_axis, chips)...  23.7 us
    pallas_call x1, Pallas kernels, _ag_sketch(): pl.pallas_call(functools.partial(_ag_sketch_kernel, chips, rb, cb, bs, su...  17.6 us

profile of v14, /device:TPU:93, one launch (start us, length us, event | category | flops | bytes accessed | tf_op | source)
XLA Modules:
  0.0 111.8 jit_solution(15287985864947055029)
XLA Ops:
  0.6 17.6 %shard_map.50 = f32[2,256,1024]{2,1,0:T(8,128)} custom-call(s32[8,8]{1,0:T(8,128)} %mask_ref.3, bf16[16,2048]{1,0:T(8,128)(2,1)} %bitcast.9, bf16[2048,2048]{1,0:T(8,128)(2,1)} %g_hbm.3), custom_call_target="tpu_custom_call" | custom-call | tf_op jit(solution)/shard_map/pallas_call | solution.py:483
  18.3 67.6 %shard_map.51 = (f32[16,2048]{1,0:T(8,128)}, f32[256,2048]{1,0:T(8,128)}) custom-call(s32[8,8]{1,0:T(8,128)} %mask_ref.3, f32[2,16,16,1024]{3,2,1,0:T(8,128)} %bitcast.5, bf16[2048,2048]{1,0:T(8,128)(2,1)} %g_hbm.3), custom_call_target="tpu_custom_call" | custom-call | tf_op jit(solution)/shard_map/pallas_call | solution.py:267
  85.8 0.0 copy-start
  85.9 23.7 %shard_map.52 = f32[16,2048]{1,0:T(8,128)} custom-call(f32[8,2,16,2048]{3,2,1,0:T(8,128)} %bitcast.6), custom_call_target="tpu_custom_call" | custom-call | tf_op jit(solution)/shard_map/pallas_call | solution.py:312
  109.5 0.0 copy-done
  109.5 0.7 copy.7
  110.2 1.6 %copy.8 = f32[2048,16]{0,1:T(8,128)} copy(f32[2048,16]{0,1:T(8,128)} %bitcast.7) | data formatting | bytes 262144
Async XLA Ops:
  85.8 23.7 %copy-start = (f32[16,2048]{1,0:T(8,128)S(1)}, f32[16,2048]{1,0:T(8,128)}, u32[]{:S(2)}) copy-start(f32[16,2048]{1,0:T(8,128)} %get-tuple-element.4) | copy-start | bytes 393220

commit v15 on v14

--- a/solution.py
+++ b/solution.py
@@ -236,25 +236,35 @@
         copy.wait_send()
 
 
-def _ar_kernel(axis, other_axis, chips, rb, cb, bs, mask_ref, x_ref, g_hbm, o_ref, t_ref,
-               g_vmem, g_sem, l_all, low, *scratch):
+def _ar_kernel(axis, other_axis, chips, row_chips, rb, cb, bs, mask_ref, x_ref, g_hbm, o_ref, a_ref,
+               g_vmem, g_sem, l_all, low, t_ref, *scratch):
+    row_scratch = scratch[21:]
     load = pltpu.make_async_copy(g_hbm, g_vmem, g_sem.at[0])
     load.start()
     me = lax.axis_index(axis)
     other = lax.axis_index(other_axis)
-    chip, core = _row_greet(axis, me, other, chips)
+    chip, core = me // 2, lax.rem(me, 2)
+    row_chip, row_core = other // 2, lax.rem(other, 2)
+    barrier = pltpu.get_barrier_semaphore()
+    for ax, mine, group, bit, count in ((axis, other, chip, core, chips), (other_axis, me, row_chip, row_core, row_chips)):
+        pl.semaphore_signal(barrier, 1, device_id=_peer(ax, mine, group * 2 + 1 - bit), device_id_type=MESH)
+        for d in range(1, count):
+            peer = lax.rem(group + d, count) * 2 + bit
+            pl.semaphore_signal(barrier, 1, device_id=_peer(ax, mine, peer), device_id_type=MESH)
+    pl.semaphore_wait(barrier, chips + row_chips)
     _mixed_rs_body(axis, other, chips, chip, core, x_ref, o_ref, *scratch[:14])
     low[...] = o_ref[...].astype(low.dtype)
-    _ag_body(axis, other, chips, chip, core, low, l_all, *scratch[14:])
+    _ag_body(axis, other, chips, chip, core, low, l_all, *scratch[14:21])
     k = l_all.shape[0] * l_all.shape[1] * l_all.shape[2]
     lowered = l_all[...].reshape(k, l_all.shape[3])
     load.wait()
     for j in range(cb):
         keep = _mask_lanes(mask_ref, rb, bs, lowered.shape[1], col=j)
         masked = jnp.where(keep, lowered, jnp.zeros_like(lowered))
-        t_ref[:, j * bs:(j + 1) * bs] = jnp.dot(
+        t_ref[:, :, :, j * bs:(j + 1) * bs] = jnp.dot(
             masked, g_vmem[:, j * bs:(j + 1) * bs], preferred_element_type=jnp.float32
-        )
+        ).reshape(t_ref.shape[0], 2, t_ref.shape[2], bs)
+    _rs_body(other_axis, me, row_chips, row_chip, row_core, t_ref, a_ref, *row_scratch)
 
 
 def _all_reduce_adjoint(x, mask, green, axis, other_axis, collective_id):
@@ -264,11 +274,14 @@
     low = jnp.bfloat16
     rb, cb = mask.shape
     bs = green.shape[0] // rb
-    return pl.pallas_call(
-        functools.partial(_ar_kernel, axis, other_axis, chips, rb, cb, bs),
+    row_chips = lax.axis_size(other_axis) // 2
+    k_rows = n * rows // (2 * row_chips)
+    cols = green.shape[1]
+    return pl.pallas_call(
+        functools.partial(_ar_kernel, axis, other_axis, chips, row_chips, rb, cb, bs),
         out_shape=(
             jax.ShapeDtypeStruct((rows, width), x.dtype),
-            jax.ShapeDtypeStruct((n * rows, green.shape[1]), jnp.float32),
+            jax.ShapeDtypeStruct((k_rows, cols), jnp.float32),
         ),
         in_specs=[
             pl.BlockSpec(memory_space=pltpu.SMEM),
@@ -281,6 +294,7 @@
             pltpu.SemaphoreType.DMA((1,)),
             pltpu.VMEM((chips, 2, rows, width), low),
             pltpu.VMEM((rows, width), low),
+            pltpu.VMEM((row_chips, 2, k_rows, cols), jnp.float32),
             pltpu.VMEM((chips, rows, half), x.dtype),
             pltpu.VMEM((chips - 1, rows, half), x.dtype),
             pltpu.VMEM((chips - 1, rows, half), x.dtype),
@@ -302,6 +316,13 @@
             pltpu.SemaphoreType.DMA((chips,)),
             pltpu.SemaphoreType.DMA((chips - 1,)),
             pltpu.SemaphoreType.DMA((chips - 1,)),
+            pltpu.VMEM((row_chips, k_rows, cols), jnp.float32),
+            pltpu.VMEM((row_chips - 1, k_rows, cols), jnp.float32),
+            pltpu.VMEM((row_chips - 1, k_rows, cols), jnp.float32),
+            pltpu.SemaphoreType.DMA((row_chips,)),
+            pltpu.SemaphoreType.DMA((row_chips,)),
+            pltpu.SemaphoreType.DMA((row_chips - 1,)),
+            pltpu.SemaphoreType.DMA((row_chips - 1,)),
         ],
         compiler_params=pltpu.CompilerParams(collective_id=collective_id, has_side_effects=True),
     )(mask, x, green)
@@ -510,10 +531,9 @@
     n_col = lax.axis_size("col")
     partial_t = _ag_sketch(probes.T, mask, green, n_row // 2, 3)
     k = partial_t.shape[1]
-    sketch_t, term_t = _all_reduce_adjoint(
+    sketch_t, adjoint_t = _all_reduce_adjoint(
         partial_t.reshape(2, n_col, k // n_col, -1), mask, green, "col", "row", 0
     )
-    adjoint_t = _row_reduce_scatter(term_t.reshape(n_row // 2, 2, k // n_row, -1), "row", "col", 2)
     return (sketch_t.T, adjoint_t.T)
 
 

time: 113 us -> 108 us (0.956)
  Pallas kernels: 109 us -> 103 us
    pallas_call x2 -> x1, Pallas kernels: 91.2 us -> 85.3 us  [_all_reduce_adjoint(): pl.pallas_call(functools.partial(_ar_kernel, axis, other_axis, chips, row...]
    unnamed x4 -> x2, local copies, waits for them, and re-layouts: 2.23 us -> 3.14 us
where the time goes in v15:
time: 108 us; the launch traced here: 107 us
  Pallas kernels  103 us (95%)
  local copies, waits for them, and re-layouts  3.14 us (3%)
    pallas_call x1, Pallas kernels, _all_reduce_adjoint(): pl.pallas_call(functools.partial(_ar_kernel, axis, other_axis, chips, row...  85.3 us
    pallas_call x1, Pallas kernels, _ag_sketch(): pl.pallas_call(functools.partial(_ag_sketch_kernel, chips, rb, cb, bs, su...  17.7 us
    unnamed x2, local copies, waits for them, and re-layouts  3.14 us

profile of v15, /device:TPU:93, one launch (start us, length us, event | category | flops | bytes accessed | tf_op | source)
XLA Modules:
  0.0 106.7 jit_solution(3641260596192827269)
XLA Ops:
  0.6 17.7 %shard_map.50 = f32[2,256,1024]{2,1,0:T(8,128)} custom-call(s32[8,8]{1,0:T(8,128)} %mask_ref.3, bf16[16,2048]{1,0:T(8,128)(2,1)} %bitcast.7, bf16[2048,2048]{1,0:T(8,128)(2,1)} %g_hbm.3), custom_call_target="tpu_custom_call" | custom-call | tf_op jit(solution)/shard_map/pallas_call | solution.py:504
  18.3 85.3 %shard_map.51 = (f32[16,2048]{1,0:T(8,128)}, f32[16,2048]{1,0:T(8,128)}) custom-call(s32[8,8]{1,0:T(8,128)} %mask_ref.3, f32[2,16,16,1024]{3,2,1,0:T(8,128)} %bitcast.4, bf16[2048,2048]{1,0:T(8,128)(2,1)} %g_hbm.3), custom_call_target="tpu_custom_call" | custom-call | tf_op jit(solution)/shard_map/pallas_call | solution.py:280
  103.6 1.6 %copy.7 = f32[2048,16]{0,1:T(8,128)} copy(f32[2048,16]{0,1:T(8,128)} %bitcast.6) | data formatting | bytes 262144
  105.1 1.6 %copy.8 = f32[2048,16]{0,1:T(8,128)} copy(f32[2048,16]{0,1:T(8,128)} %bitcast.5) | data formatting | bytes 262144

commit v16 on v15

--- a/solution.py
+++ b/solution.py
@@ -236,9 +236,9 @@
         copy.wait_send()
 
 
-def _ar_kernel(axis, other_axis, chips, row_chips, rb, cb, bs, mask_ref, x_ref, g_hbm, o_ref, a_ref,
-               g_vmem, g_sem, l_all, low, t_ref, *scratch):
-    row_scratch = scratch[21:]
+def _ar_kernel(axis, other_axis, chips, row_chips, rb, cb, bs, mask_ref, p_ref, g_hbm, o_ref, a_ref,
+               g_vmem, g_sem, l_all, low, t_ref, x_ref, p_all, *scratch):
+    row_scratch = scratch[21:28]
     load = pltpu.make_async_copy(g_hbm, g_vmem, g_sem.at[0])
     load.start()
     me = lax.axis_index(axis)
@@ -252,12 +252,22 @@
             peer = lax.rem(group + d, count) * 2 + bit
             pl.semaphore_signal(barrier, 1, device_id=_peer(ax, mine, peer), device_id_type=MESH)
     pl.semaphore_wait(barrier, chips + row_chips)
+    _ag_body(other_axis, me, row_chips, row_chip, row_core, p_ref, p_all, *scratch[28:])
+    k = p_all.shape[0] * p_all.shape[1] * p_all.shape[2]
+    probes_t = p_all[...].reshape(k, p_all.shape[3])
+    load.wait()
+    sub = x_ref.shape[-1] // bs
+    for h in range(rb):
+        keep = _mask_lanes(mask_ref, cb, bs, probes_t.shape[1], row=h)
+        p = jnp.where(keep, probes_t, jnp.zeros_like(probes_t))
+        x_ref[h // sub, :, :, (h % sub) * bs:(h % sub + 1) * bs] = lax.dot_general(
+            p, g_vmem[h * bs:(h + 1) * bs, :], (((1,), (1,)), ((), ())), preferred_element_type=jnp.float32
+        ).reshape(x_ref.shape[1], x_ref.shape[2], bs)
     _mixed_rs_body(axis, other, chips, chip, core, x_ref, o_ref, *scratch[:14])
     low[...] = o_ref[...].astype(low.dtype)
     _ag_body(axis, other, chips, chip, core, low, l_all, *scratch[14:21])
     k = l_all.shape[0] * l_all.shape[1] * l_all.shape[2]
     lowered = l_all[...].reshape(k, l_all.shape[3])
-    load.wait()
     for j in range(cb):
         keep = _mask_lanes(mask_ref, rb, bs, lowered.shape[1], col=j)
         masked = jnp.where(keep, lowered, jnp.zeros_like(lowered))
@@ -267,8 +277,11 @@
     _rs_body(other_axis, me, row_chips, row_chip, row_core, t_ref, a_ref, *row_scratch)
 
 
-def _all_reduce_adjoint(x, mask, green, axis, other_axis, collective_id):
-    _, n, rows, half = x.shape
+def _all_reduce_adjoint(probes_t, mask, green, axis, other_axis, collective_id):
+    n = lax.axis_size(axis)
+    rows = probes_t.shape[0] * lax.axis_size(other_axis) // n
+    half = green.shape[0] // 2
+    x = jax.ShapeDtypeStruct((2, n, rows, half), jnp.float32)
     chips = n // 2
     width = 2 * half
     low = jnp.bfloat16
@@ -280,7 +293,7 @@
     return pl.pallas_call(
         functools.partial(_ar_kernel, axis, other_axis, chips, row_chips, rb, cb, bs),
         out_shape=(
-            jax.ShapeDtypeStruct((rows, width), x.dtype),
+            jax.ShapeDtypeStruct((rows, width), jnp.float32),
             jax.ShapeDtypeStruct((k_rows, cols), jnp.float32),
         ),
         in_specs=[
@@ -295,6 +308,8 @@
             pltpu.VMEM((chips, 2, rows, width), low),
             pltpu.VMEM((rows, width), low),
             pltpu.VMEM((row_chips, 2, k_rows, cols), jnp.float32),
+            pltpu.VMEM((2, n, rows, half), jnp.float32),
+            pltpu.VMEM((row_chips, 2) + probes_t.shape, probes_t.dtype),
             pltpu.VMEM((chips, rows, half), x.dtype),
             pltpu.VMEM((chips - 1, rows, half), x.dtype),
             pltpu.VMEM((chips - 1, rows, half), x.dtype),
@@ -323,9 +338,16 @@
             pltpu.SemaphoreType.DMA((row_chips,)),
             pltpu.SemaphoreType.DMA((row_chips - 1,)),
             pltpu.SemaphoreType.DMA((row_chips - 1,)),
+            pltpu.VMEM(probes_t.shape, probes_t.dtype),
+            pltpu.VMEM((row_chips - 1,) + probes_t.shape, probes_t.dtype),
+            pltpu.VMEM((row_chips - 1,) + probes_t.shape, probes_t.dtype),
+            pltpu.SemaphoreType.DMA((row_chips,)),
+            pltpu.SemaphoreType.DMA((row_chips,)),
+            pltpu.SemaphoreType.DMA((row_chips - 1,)),
+            pltpu.SemaphoreType.DMA((row_chips - 1,)),
         ],
         compiler_params=pltpu.CompilerParams(collective_id=collective_id, has_side_effects=True),
-    )(mask, x, green)
+    )(mask, probes_t, green)
 
 
 def _row_reduce_scatter(x, axis, other_axis, collective_id):
@@ -529,11 +551,7 @@
 def local(green, mask, probes):
     n_row = lax.axis_size("row")
     n_col = lax.axis_size("col")
-    partial_t = _ag_sketch(probes.T, mask, green, n_row // 2, 3)
-    k = partial_t.shape[1]
-    sketch_t, adjoint_t = _all_reduce_adjoint(
-        partial_t.reshape(2, n_col, k // n_col, -1), mask, green, "col", "row", 0
-    )
+    sketch_t, adjoint_t = _all_reduce_adjoint(probes.T, mask, green, "col", "row", 0)
     return (sketch_t.T, adjoint_t.T)
 
 

time: 108 us -> 104 us (0.963)
  Pallas kernels: 103 us -> 99.4 us
    pallas_call x1 -> x0, Pallas kernels: 17.7 us -> none  [_ag_sketch(): pl.pallas_call(functools.partial(_ag_sketch_kernel, chips, rb, cb, bs, su...]
    pallas_call x1, Pallas kernels: 85.3 us -> 99.4 us  [_all_reduce_adjoint(): pl.pallas_call(functools.partial(_ar_kernel, axis, other_axis, chips, row...]
where the time goes in v16:
time: 104 us; the launch traced here: 103 us
  Pallas kernels  99.4 us (96%)
  local copies, waits for them, and re-layouts  3.14 us (3%)
    pallas_call x1, Pallas kernels, _all_reduce_adjoint(): pl.pallas_call(functools.partial(_ar_kernel, axis, other_axis, chips, row...  99.4 us
    unnamed x2, local copies, waits for them, and re-layouts  3.14 us

profile of v16, /device:TPU:93, one launch (start us, length us, event | category | flops | bytes accessed | tf_op | source)
XLA Modules:
  0.0 103.2 jit_solution(12664496187707635722)
XLA Ops:
  0.6 99.4 %shard_map.50 = (f32[16,2048]{1,0:T(8,128)}, f32[16,2048]{1,0:T(8,128)}) custom-call(s32[8,8]{1,0:T(8,128)} %mask_ref.1, bf16[16,2048]{1,0:T(8,128)(2,1)} %bitcast.5, bf16[2048,2048]{1,0:T(8,128)(2,1)} %g_hbm.1), custom_call_target="tpu_custom_call" | custom-call | tf_op jit(solution)/shard_map/pallas_call | solution.py:293
  100.0 1.6 %copy.7 = f32[2048,16]{0,1:T(8,128)} copy(f32[2048,16]{0,1:T(8,128)} %bitcast.4) | data formatting | bytes 262144
  101.6 1.6 %copy.8 = f32[2048,16]{0,1:T(8,128)} copy(f32[2048,16]{0,1:T(8,128)} %bitcast.3) | data formatting | bytes 262144

commit v17 on v16

--- a/solution.py
+++ b/solution.py
@@ -175,7 +175,7 @@
 
 
 def _mixed_rs_body(axis, other, chips, chip, core, x_ref, o_ref, ra1, ma, ra2, rb1, mb, rb2,
-                   sa1, qa1, sa2, qa2, sb1, qb1, sb2, qb2):
+                   sa1, qa1, sa2, qa2, sb1, qb1, sb2, qb2, between=None):
     sib = _peer(axis, other, chip * 2 + 1 - core)
     width = x_ref.shape[-1]
     a1 = []
@@ -187,6 +187,8 @@
         )
         copy.start()
         a1.append(copy)
+    if between is not None:
+        between()
     b1 = []
     for d in range(1, chips):
         target = lax.rem(chip + d, chips)
@@ -257,13 +259,17 @@
     probes_t = p_all[...].reshape(k, p_all.shape[3])
     load.wait()
     sub = x_ref.shape[-1] // bs
-    for h in range(rb):
-        keep = _mask_lanes(mask_ref, cb, bs, probes_t.shape[1], row=h)
-        p = jnp.where(keep, probes_t, jnp.zeros_like(probes_t))
-        x_ref[h // sub, :, :, (h % sub) * bs:(h % sub + 1) * bs] = lax.dot_general(
-            p, g_vmem[h * bs:(h + 1) * bs, :], (((1,), (1,)), ((), ())), preferred_element_type=jnp.float32
-        ).reshape(x_ref.shape[1], x_ref.shape[2], bs)
-    _mixed_rs_body(axis, other, chips, chip, core, x_ref, o_ref, *scratch[:14])
+
+    def sketch(step):
+        for h in range(step * sub, (step + 1) * sub):
+            keep = _mask_lanes(mask_ref, cb, bs, probes_t.shape[1], row=h)
+            p = jnp.where(keep, probes_t, jnp.zeros_like(probes_t))
+            x_ref[step, :, :, (h % sub) * bs:(h % sub + 1) * bs] = lax.dot_general(
+                p, g_vmem[h * bs:(h + 1) * bs, :], (((1,), (1,)), ((), ())), preferred_element_type=jnp.float32
+            ).reshape(x_ref.shape[1], x_ref.shape[2], bs)
+
+    sketch(0)
+    _mixed_rs_body(axis, other, chips, chip, core, x_ref, o_ref, *scratch[:14], between=lambda: sketch(1))
     low[...] = o_ref[...].astype(low.dtype)
     _ag_body(axis, other, chips, chip, core, low, l_all, *scratch[14:21])
     k = l_all.shape[0] * l_all.shape[1] * l_all.shape[2]

time: 104 us -> 104 us (level)
  no operation moved by 1% of the time
where the time goes in v17:
time: 104 us; the launch traced here: 103 us
  Pallas kernels  99.6 us (96%)
  local copies, waits for them, and re-layouts  3.14 us (3%)
    pallas_call x1, Pallas kernels, _all_reduce_adjoint(): pl.pallas_call(functools.partial(_ar_kernel, axis, other_axis, chips, row...  99.6 us
    unnamed x2, local copies, waits for them, and re-layouts  3.14 us

profile of v17, /device:TPU:93, one launch (start us, length us, event | category | flops | bytes accessed | tf_op | source)
XLA Modules:
  0.0 103.4 jit_solution(7841570605377110002)
XLA Ops:
  0.6 99.6 %shard_map.50 = (f32[16,2048]{1,0:T(8,128)}, f32[16,2048]{1,0:T(8,128)}) custom-call(s32[8,8]{1,0:T(8,128)} %mask_ref.1, bf16[16,2048]{1,0:T(8,128)(2,1)} %bitcast.5, bf16[2048,2048]{1,0:T(8,128)(2,1)} %g_hbm.1), custom_call_target="tpu_custom_call" | custom-call | tf_op jit(solution)/shard_map/pallas_call | solution.py:299
  100.2 1.6 %copy.7 = f32[2048,16]{0,1:T(8,128)} copy(f32[2048,16]{0,1:T(8,128)} %bitcast.4) | data formatting | bytes 262144
  101.8 1.6 %copy.8 = f32[2048,16]{0,1:T(8,128)} copy(f32[2048,16]{0,1:T(8,128)} %bitcast.3) | data formatting | bytes 262144

commit v18 on v17

--- a/solution.py
+++ b/solution.py
@@ -91,7 +91,7 @@
     _rs_body(axis, other, chips, chip, core, x_ref, o_ref, recv1, mid, recv2, s1, r1, s2, r2)
 
 
-def _rs_body(axis, other, chips, chip, core, x_ref, o_ref, recv1, mid, recv2, s1, r1, s2, r2):
+def _rs_body(axis, other, chips, chip, core, x_ref, o_ref, recv1, mid, recv2, s1, r1, s2, r2, between=None):
     sib = _peer(axis, other, chip * 2 + 1 - core)
     first = []
     for d in list(range(1, chips)) + [0]:
@@ -106,6 +106,8 @@
         )
         copy.start()
         first.append(copy)
+    if between is not None:
+        between()
     sends = []
     for d in range(1, chips):
         target = lax.rem(chip + d, chips)
@@ -272,15 +274,20 @@
     _mixed_rs_body(axis, other, chips, chip, core, x_ref, o_ref, *scratch[:14], between=lambda: sketch(1))
     low[...] = o_ref[...].astype(low.dtype)
     _ag_body(axis, other, chips, chip, core, low, l_all, *scratch[14:21])
-    k = l_all.shape[0] * l_all.shape[1] * l_all.shape[2]
-    lowered = l_all[...].reshape(k, l_all.shape[3])
-    for j in range(cb):
-        keep = _mask_lanes(mask_ref, rb, bs, lowered.shape[1], col=j)
-        masked = jnp.where(keep, lowered, jnp.zeros_like(lowered))
-        t_ref[:, :, :, j * bs:(j + 1) * bs] = jnp.dot(
-            masked, g_vmem[:, j * bs:(j + 1) * bs], preferred_element_type=jnp.float32
-        ).reshape(t_ref.shape[0], 2, t_ref.shape[2], bs)
-    _rs_body(other_axis, me, row_chips, row_chip, row_core, t_ref, a_ref, *row_scratch)
+    def adjoint(bit):
+        k = l_all.shape[0] * l_all.shape[1] * l_all.shape[2]
+        full = l_all[...].reshape(t_ref.shape[0], 2, k // (2 * t_ref.shape[0]), l_all.shape[3])
+        lowered = jnp.where(bit == 0, full[:, 0], full[:, 1]).reshape(k // 2, l_all.shape[3])
+        for j in range(cb):
+            keep = _mask_lanes(mask_ref, rb, bs, lowered.shape[1], col=j)
+            masked = jnp.where(keep, lowered, jnp.zeros_like(lowered))
+            t_ref[:, bit, :, j * bs:(j + 1) * bs] = jnp.dot(
+                masked, g_vmem[:, j * bs:(j + 1) * bs], preferred_element_type=jnp.float32
+            ).reshape(t_ref.shape[0], t_ref.shape[2], bs)
+
+    adjoint(1 - row_core)
+    _rs_body(other_axis, me, row_chips, row_chip, row_core, t_ref, a_ref, *row_scratch,
+             between=lambda: adjoint(row_core))
 
 
 def _all_reduce_adjoint(probes_t, mask, green, axis, other_axis, collective_id):

time: 104 us -> 105 us (level)
  no operation moved by 1% of the time
where the time goes in v18:
time: 105 us; the launch traced here: 104 us
  Pallas kernels  100 us (95%)
  local copies, waits for them, and re-layouts  3.14 us (3%)
    pallas_call x1, Pallas kernels, _all_reduce_adjoint(): pl.pallas_call(functools.partial(_ar_kernel, axis, other_axis, chips, row...  100 us
    unnamed x2, local copies, waits for them, and re-layouts  3.14 us

profile of v18, /device:TPU:93, one launch (start us, length us, event | category | flops | bytes accessed | tf_op | source)
XLA Modules:
  0.0 104.1 jit_solution(1899815586880764318)
XLA Ops:
  0.6 100.3 %shard_map.50 = (f32[16,2048]{1,0:T(8,128)}, f32[16,2048]{1,0:T(8,128)}) custom-call(s32[8,8]{1,0:T(8,128)} %mask_ref.1, bf16[16,2048]{1,0:T(8,128)(2,1)} %bitcast.5, bf16[2048,2048]{1,0:T(8,128)(2,1)} %g_hbm.1), custom_call_target="tpu_custom_call" | custom-call | tf_op jit(solution)/shard_map/pallas_call | solution.py:306
  100.9 1.6 %copy.7 = f32[2048,16]{0,1:T(8,128)} copy(f32[2048,16]{0,1:T(8,128)} %bitcast.4) | data formatting | bytes 262144
  102.5 1.6 %copy.8 = f32[2048,16]{0,1:T(8,128)} copy(f32[2048,16]{0,1:T(8,128)} %bitcast.3) | data formatting | bytes 262144

commit v19 on v17

--- a/solution.py
+++ b/solution.py
@@ -178,17 +178,6 @@
                    sa1, qa1, sa2, qa2, sb1, qb1, sb2, qb2, between=None):
     sib = _peer(axis, other, chip * 2 + 1 - core)
     width = x_ref.shape[-1]
-    a1 = []
-    for d in list(range(1, chips)) + [0]:
-        target = lax.rem(chip + d, chips)
-        copy = pltpu.make_async_remote_copy(
-            src_ref=x_ref.at[0, target * 2 + 1 - core], dst_ref=ra1.at[d], send_sem=sa1.at[d],
-            recv_sem=qa1.at[d], device_id=sib, device_id_type=MESH,
-        )
-        copy.start()
-        a1.append(copy)
-    if between is not None:
-        between()
     b1 = []
     for d in range(1, chips):
         target = lax.rem(chip + d, chips)
@@ -200,6 +189,17 @@
             )
             copy.start()
             b1.append(copy)
+    if between is not None:
+        between()
+    a1 = []
+    for d in list(range(1, chips)) + [0]:
+        target = lax.rem(chip + d, chips)
+        copy = pltpu.make_async_remote_copy(
+            src_ref=x_ref.at[0, target * 2 + 1 - core], dst_ref=ra1.at[d], send_sem=sa1.at[d],
+            recv_sem=qa1.at[d], device_id=sib, device_id_type=MESH,
+        )
+        copy.start()
+        a1.append(copy)
     a2 = []
     for d in range(1, chips):
         target = lax.rem(chip + d, chips)
@@ -268,8 +268,8 @@
                 p, g_vmem[h * bs:(h + 1) * bs, :], (((1,), (1,)), ((), ())), preferred_element_type=jnp.float32
             ).reshape(x_ref.shape[1], x_ref.shape[2], bs)
 
-    sketch(0)
-    _mixed_rs_body(axis, other, chips, chip, core, x_ref, o_ref, *scratch[:14], between=lambda: sketch(1))
+    sketch(1)
+    _mixed_rs_body(axis, other, chips, chip, core, x_ref, o_ref, *scratch[:14], between=lambda: sketch(0))
     low[...] = o_ref[...].astype(low.dtype)
     _ag_body(axis, other, chips, chip, core, low, l_all, *scratch[14:21])
     k = l_all.shape[0] * l_all.shape[1] * l_all.shape[2]

time: 104 us -> 103 us (level)
  Pallas kernels: 99.6 us -> 98.3 us
    pallas_call x1, Pallas kernels: 99.6 us -> 98.3 us  [_all_reduce_adjoint(): pl.pallas_call(functools.partial(_ar_kernel, axis, other_axis, chips, row...]
where the time goes in v19:
time: 103 us; the launch traced here: 102 us
  Pallas kernels  98.3 us (95%)
  local copies, waits for them, and re-layouts  3.14 us (3%)
    pallas_call x1, Pallas kernels, _all_reduce_adjoint(): pl.pallas_call(functools.partial(_ar_kernel, axis, other_axis, chips, row...  98.3 us
    unnamed x2, local copies, waits for them, and re-layouts  3.14 us

profile of v19, /device:TPU:93, one launch (start us, length us, event | category | flops | bytes accessed | tf_op | source)
XLA Modules:
  0.0 102.1 jit_solution(1017989888178990544)
XLA Ops:
  0.6 98.3 %shard_map.50 = (f32[16,2048]{1,0:T(8,128)}, f32[16,2048]{1,0:T(8,128)}) custom-call(s32[8,8]{1,0:T(8,128)} %mask_ref.1, bf16[16,2048]{1,0:T(8,128)(2,1)} %bitcast.5, bf16[2048,2048]{1,0:T(8,128)(2,1)} %g_hbm.1), custom_call_target="tpu_custom_call" | custom-call | tf_op jit(solution)/shard_map/pallas_call | solution.py:299
  98.9 1.6 %copy.7 = f32[2048,16]{0,1:T(8,128)} copy(f32[2048,16]{0,1:T(8,128)} %bitcast.4) | data formatting | bytes 262144
  100.5 1.6 %copy.8 = f32[2048,16]{0,1:T(8,128)} copy(f32[2048,16]{0,1:T(8,128)} %bitcast.3) | data formatting | bytes 262144
